TPU v7x, 256 devices: a whole 4x4x8 slice. The times are simulated.
256 devices in a mesh: row: 16 (over x_lo, z), col: 16 (over x_hi, y, core).
Axes of the slice: x: 4 (x_hi: 2, x_lo: 2; x = x_hi * 2 + x_lo), y: 4, z: 8, core: 2. Of those that a mesh axis runs over, the one named last changes fastest.
Arguments:
- ham_blocks: bfloat16 [128, 4, 128, 128], P('row'), may hold values from -0.25 to 0.25
- ham_index: int32 [128, 4], P('row'), may hold values from -1 to 127, as said below
- coef_blocks: bfloat16 [64, 16, 128, 128], P('col', 'row'), may hold values from -0.5 to 0.5
- coef_index: int32 [64, 16], P('col', 'row'), may hold values from 0 to 127, as said below
- slab_blocks: bfloat16 [16, 16, 128, 128], P('row', 'col'), may hold values from -0.5 to 0.5
- slab_index: int32 [16, 16], P('row', 'col'), may hold values from 0 to 127, as said below
- pattern_index: int32 [16, 32], P('row', 'col'), may hold values from 0 to 63, as said below
Outputs:
- reduced_blocks: bfloat16 [16, 32, 128, 128], P('row', 'col')
Inputs may be any that keep to these rules, and one draw needn't show every extreme that they name: `ham_index`: each row lists its stored block columns first, all distinct, then -1 in every unused slot; a row holds 1 to 4 stored blocks, some row holds 4 and some row only one. `coef_index`: each row names 16 distinct orbital blocks. `slab_index`: each row names 16 distinct orbital blocks. `pattern_index`: entry k of a row names a block among (k // 2) * 4 to (k // 2) * 4 + 3.
All inputs are finite; a program needn't handle non-finite values.
Results may differ from a plain program's by a relative error of at most 0.0049.
Values may be sent and summed in bfloat16 or wider, within the bound.
No kernel may reach another device: no remote copies, remote signals or barrier semaphores. Data moves between devices by JAX's collectives and lax.ppermute only.
A program may use at most 128 MiB of HBM per device.

v0:
```python
import jax
import jax.numpy as jnp
from jax import lax
from jax.experimental import pallas as pl
from jax.experimental.pallas import tpu as pltpu
from jax.sharding import PartitionSpec as P


BF = jnp.bfloat16
F32 = jnp.float32
I32 = jnp.int32
COLS = 16
PLACES = ((0, 0), (1, 0), (0, 1), (1, 1), (0, 3), (1, 3), (0, 2), (1, 2))
SMEM = pl.BlockSpec(memory_space=pltpu.SMEM)
VMEM = pl.BlockSpec(memory_space=pltpu.VMEM)
ANY = pl.BlockSpec(memory_space=pl.ANY)


def iota(shape, dim):
    return lax.broadcasted_iota(I32, shape, dim)


def hot(cond):
    return jnp.where(cond, 1.0, 0.0).astype(BF)


def dot(a, b):
    return jnp.dot(a, b, preferred_element_type=F32)


def split_kernel(coef_idx, ham, coef, slab, send, own, swap, part, turned, sem):
    col = lax.axis_index("col")
    chip, core = col // 2, col % 2
    copy = pltpu.make_async_copy(ham.at[:, :, pl.ds(pl.multiple_of(chip * 16, 16), 16), :], part, sem)
    copy.start()
    for j in range(4):
        turned[j] = coef[j, 0].T
    own[...] = turned[:, pl.ds(pl.multiple_of(core * 64, 64), 64), :]
    swap[0:256, :] = turned[:, pl.ds(pl.multiple_of((1 - core) * 64, 64), 64), :].reshape(256, 128)
    swap[256:384, :] = slab[0, 0]
    lane = iota((16, 128), 1)
    names = jnp.zeros((16, 128), I32)
    for j in range(4):
        names = jnp.where(lane == j, coef_idx[j, 0], names)
    swap[384:400, :] = names.astype(F32).astype(BF)
    a, b = iota((128, 128), 0), iota((128, 128), 1)
    order = hot((a // 8 == b % 16) & (a % 8 == b // 16))
    first = hot((b < 64) & (a == b + 64 * core))
    second = hot((b >= 64) & (a == b - 64 + 64 * core))
    copy.wait()
    for s in range(2):
        left = part[:, 2 * s].reshape(128, 128)
        right = part[:, 2 * s + 1].reshape(128, 128)
        half = (dot(left, first) + dot(right, second)).astype(BF)
        send[:, :, s * 128 : (s + 1) * 128] = dot(order, half).reshape(16, 8, 128).astype(BF)


def stamp_kernel(ham_idx, coef_idx, named, swapped, parts, send):
    send[:, :, 0:256] = parts[...]
    lane, line = iota((8, 128), 1), iota((8, 128), 0)
    meta = jnp.zeros((8, 128), I32)
    for p in range(8):
        for k in range(4):
            meta = jnp.where((line == p) & (lane == k), ham_idx[p, k], meta)
    for j in range(4):
        meta = jnp.where(lane == 4 + j, coef_idx[j, 0], meta)
    a, b = iota((128, 128), 0), iota((128, 128), 1)
    flat = named[...].astype(F32).reshape(128, 128).astype(BF)
    slabs = (b >= 16) & (b < 32)
    pats = (b >= 32) & (b < 64)
    src = jnp.where(slabs, 0, 1 + b % 2)
    at = jnp.where(slabs, b - 16, (b - 32) // 2)
    picked = dot(flat, hot((slabs | pats) & (a == src)))
    line_all = jnp.sum(jnp.where(a == 8 * at, picked, 0.0), axis=0, keepdims=True)
    others = dot(swapped[384:400, :], hot((b >= 8) & (b < 12) & (a == b - 8)))[0:8]
    meta = meta.astype(F32) + line_all + others
    send[:, :, 256:384] = jnp.broadcast_to(meta.astype(BF)[None], (16, 8, 128))


def pick_kernel(got, send):
    pieces = got[:, :, 0:256].astype(F32).reshape(128, 256).astype(BF)
    flat = got[:, :, 256:384].astype(F32).reshape(128, 128).astype(BF)
    a, b = iota((16, 128), 0), iota((16, 128), 1)
    names = lax.dot_general(hot(b == 16 + a), flat, (((1,), (1,)), ((), ())), preferred_element_type=F32)
    lane = b.astype(F32)
    picks = jnp.concatenate(
        [jnp.where(names[:, 8 * r : 8 * r + 1] == lane, 1.0, 0.0) for r in range(16)], axis=0
    )
    send[...] = dot(picks.astype(BF), pieces).astype(BF).reshape(16, 16, 256)


def pack_kernel(got, piece):
    a, b = iota((256, 256), 0), iota((256, 256), 1)
    order = hot((a // 16 == b % 16) & (a % 16 == b // 16))
    piece[...] = dot(order, got[...].reshape(256, 256)).astype(BF).reshape(16, 16, 256)


def choose_kernel(tables, own, swapped, send, both):
    col = lax.axis_index("col")
    chip, core = col // 2, col % 2
    both[core] = own[...]
    both[1 - core] = swapped[0:256, :].reshape(4, 64, 128)
    for r in range(16):
        for i in range(4):
            at = 2 * chip + i // 2
            j = tables[r, 32 + 2 * at + i % 2] - 4 * at
            send[r, i] = both[i // 2, j]


def match_kernel(ham_names, tables, out, slots):
    row, col = lax.axis_index("row"), lax.axis_index("col")
    chip, core = col // 2, col % 2

    def clear(q, _):
        for i in range(4):
            slots[i * 128 + q] = -1
        return 0

    lax.fori_loop(0, 128, clear, 0)
    for i in range(4):
        at = 2 * chip + i // 2
        j = tables[row, 32 + 2 * at + i % 2] - 4 * at
        base = jnp.where(core == i // 2, 4, 8) + j
        for m in range(16):
            slots[i * 128 + tables[m, base]] = m

    def one(m, _):
        p = tables[row, 16 + m]
        for k in range(4):
            q = ham_names[p, k]
            for i in range(4):
                out[m * 16 + k * 4 + i] = jnp.where(q >= 0, slots[i * 128 + jnp.maximum(q, 0)], -1)
        return 0

    lax.fori_loop(0, 16, one, 0)


def product_kernel(match, coefs, *refs):
    hams, slabs, (own, send), (ham, slab, image, chosen, sems) = refs[:8], refs[8:12], refs[12:14], refs[14:]
    col = lax.axis_index("col")
    chip, core = col // 2, col % 2
    x, y = chip // 4, chip % 4
    copies = []
    for t, (dx, dy) in enumerate(PLACES):
        s = ((x + dx) % 2) * 4 + (y - dy + 4) % 4
        at = pl.ds(pl.multiple_of(s * 16, 16), 16)
        copies.append(pltpu.make_async_copy(hams[t], ham.at[:, at, :], sems.at[t]))
        if t % 2 == 0:
            for h in range(2):
                s = ((x + h) % 2) * 4 + (y - dy + 4) % 4
                copies.append(pltpu.make_async_copy(slabs[t // 2].at[h], slab.at[s], sems.at[8 + t + h]))
    for copy in copies:
        copy.start()
    for copy in copies:
        copy.wait()

    total = jnp.zeros((128, 512), F32)
    for s in range(8):
        for h in range(2):
            m = 2 * s + (core + h) % 2
            for k in range(4):
                for i in range(4):
                    slot = match[m * 16 + k * 4 + i]
                    found = coefs[jnp.maximum(slot, 0), i]
                    chosen[h, k * 64 : k * 64 + 64, i * 128 : i * 128 + 128] = jnp.where(slot >= 0, found, jnp.zeros_like(found))
            image[s, h * 128 : h * 128 + 128, :] = dot(ham[m], chosen[h]).astype(BF)
    for s in range(8):
        for h in range(2):
            total = total + dot(slab[s, h], image[s, h * 128 : h * 128 + 128, :])
    for e in range(2):
        low, high = total[:, e * 128 : e * 128 + 128], total[:, 256 + e * 128 : 384 + e * 128]
        own[e] = jnp.where(core == 0, low, high)
        send[e] = jnp.where(core == 0, high, low).astype(BF)


def shift(value, dx, dy):
    pairs = [
        (x * 8 + y * 2 + k, ((x + dx) % 2) * 8 + ((y + dy) % 4) * 2 + k)
        for x in range(2)
        for y in range(4)
        for k in range(2)
    ]
    return lax.ppermute(value, "col", pairs)


def near(value):
    return pltpu.with_memory_space_constraint(value, pltpu.VMEM)


def run(kernel, outs, specs, args, scratch=()):
    args = [near(v) if spec == "near" else v for spec, v in zip(specs, args)]
    specs = [VMEM if spec == "near" else spec for spec in specs]
    single = not isinstance(outs, list)
    outs = [outs] if single else outs
    result = pl.pallas_call(
        kernel,
        out_shape=[pltpu.VMEM(shape, kind) for shape, kind in outs],
        in_specs=specs,
        out_specs=[VMEM] * len(outs),
        scratch_shapes=scratch,
    )(*args)
    return result[0] if single else result


def body(ham_blocks, ham_index, coef_blocks, coef_index, slab_blocks, slab_index, pattern_index):
    cores = [(i, i ^ 1) for i in range(COLS)]

    names = jnp.concatenate([slab_index, pattern_index], axis=1).astype(BF)
    names = jnp.broadcast_to(jnp.pad(names, ((0, 7), (0, 125)))[None], (COLS, 8, 128))
    named = lax.all_to_all(names, "col", 0, 0)

    parts, half, swap = run(
        split_kernel,
        [((16, 8, 256), BF), ((4, 64, 128), BF), ((400, 128), BF)],
        [SMEM, ANY, VMEM, VMEM],
        [coef_index, ham_blocks, coef_blocks, slab_blocks],
        [pltpu.VMEM((8, 4, 16, 128), BF), pltpu.VMEM((4, 128, 128), BF), pltpu.SemaphoreType.DMA],
    )
    swapped = lax.ppermute(swap, "col", cores)

    stamped = run(
        stamp_kernel,
        ((16, 8, 384), BF),
        [SMEM, SMEM, "near", "near", "near"],
        [ham_index, coef_index, named, swapped, parts],
    )
    got = lax.all_to_all(stamped, "row", 0, 0)

    pair = jnp.stack([slab_blocks[0, 0], swapped[256:384]]).reshape(2, 128, 128)
    quad = jnp.stack([pair, shift(pair, 1, 0)])
    quads = [quad] + [shift(quad, 0, d) for d in (1, 3, 2)]

    picked = run(pick_kernel, ((16, 16, 256), BF), ["near"], [got])
    picks = lax.all_to_all(picked, "row", 0, 0)

    numbers = got[:, 0, 256:384].astype(I32)
    ham_names = got[:, :, 256:260].reshape(128, 4).astype(I32)
    wanted = run(
        choose_kernel,
        ((16, 4, 64, 128), BF),
        [SMEM, "near", "near"],
        [numbers, half, swapped],
        [pltpu.VMEM((2, 4, 64, 128), BF)],
    )
    wanted, picks, *quads = lax.optimization_barrier((wanted, picks, *quads))
    coefs = lax.all_to_all(wanted, "row", 0, 0)

    piece = run(pack_kernel, ((16, 16, 256), BF), ["near"], [picks])
    across = shift(piece, 1, 0)
    hams = [piece, across]
    for d in (1, 3, 2):
        hams += [shift(piece, 0, d), shift(across, 0, d)]

    match = pl.pallas_call(
        match_kernel,
        out_shape=jax.ShapeDtypeStruct((256,), I32),
        in_specs=[SMEM] * 2,
        out_specs=SMEM,
        scratch_shapes=[pltpu.SMEM((512,), I32)],
        name="match",
    )(ham_names, numbers)

    mine, other = run(
        product_kernel,
        [((2, 128, 128), F32), ((2, 128, 128), BF)],
        [SMEM] + ["near"] * 13,
        [match, coefs, *hams, *quads],
        [
            pltpu.VMEM((16, 128, 256), BF),
            pltpu.VMEM((8, 2, 128, 128), BF),
            pltpu.VMEM((8, 256, 512), BF),
            pltpu.VMEM((2, 256, 512), BF),
            pltpu.SemaphoreType.DMA((16,)),
        ],
    )
    theirs = lax.ppermute(other, "col", cores)
    return (mine + theirs.astype(F32)).astype(BF)[None]


def solution(mesh):
    placed = (
        P("row", None, None, None),
        P("row", None),
        P("col", "row", None, None),
        P("col", "row"),
        P("row", "col", None, None),
        P("row", "col"),
        P("row", "col"),
    )
    return jax.shard_map(
        body, mesh=mesh, in_specs=placed, out_specs=P("row", "col", None, None), check_vma=False
    )
```

profile of v0, /device:TPU:1, one launch (start us, length us, event | category | flops | bytes accessed | tf_op | source)
XLA Modules:
  0.0 96.5 jit_solution(6682430138019313131)
XLA Ops:
  0.0 1.3 %copy.10.coef_idx = s32[4,1]{1,0:T(4,128)} copy(s32[4,1]{0,1:T(1,128)} %param.10) | data formatting | bytes 32 | tf_op args[3]
  1.3 2.3 %shard_map.73 = (bf16[16,8,256]{2,1,0:T(8,128)(2,1)S(1)}, bf16[4,64,128]{2,1,0:T(8,128)(2,1)S(1)}, bf16[400,128]{1,0:T(8,128)(2,1)S(1)}) custom-call(s32[4,1]{1,0:T(4,128)} %copy.10.coef_idx, bf16[8,4,128,128]{3,2,1,0:T(8,128)(2,1)} %ham.1, bf16[4,1,128,128]{3,2,1,0:T(8,128)(2,1)} %coef.1, bf16[1,1,128,128]{3,2,1,0:T(8,128)(2,1)} %slab.1), custom_call_target="tpu_custom_call" | custom-call | tf_op jit(solution)/shard_map/pallas_call | solution.py:195
  3.6 3.3 %collective-permute-start = (bf16[400,128]{1,0:T(8,128)(2,1)S(1)}, bf16[400,128]{1,0:T(8,128)(2,1)S(1)}, u32[]{:S(2)}, u32[]{:S(2)}) collective-permute-start(bf16[400,128]{1,0:T(8,128)(2,1)S(1)} %get-tuple-element.16), channel_id=1, source_target_pairs={{0,1},{1,0},{2,3},{3,2},{4,5},{5,4},{6,7},{7,6},{8,9},{9,8},{10,11... | collective-permute-start | bytes 307208 | tf_op jit(solution)/shard_map/ppermute | solution.py:219
  9.0 5.5 %all-to-all-start = ((bf16[16,8,128]{2,1,0:T(8,128)(2,1)}), bf16[16,8,128]{2,1,0:T(8,128)(2,1)S(1)}, u32[]{:S(2)}, u32[]{:S(2)}) async-start(bf16[16,8,128]{2,1,0:T(8,128)(2,1)} %broadcast_in_dim.4), calls=%async_computation | async-start | bytes 65536 | tf_op jit(solution)/shard_map/all_to_all | solution.py:210
  14.4 0.7 copy.9.ham_idx
  15.1 6.6 %all-to-all-done.named = bf16[16,8,128]{2,1,0:T(8,128)(2,1)S(1)} async-done(((bf16[16,8,128]{2,1,0:T(8,128)(2,1)}), bf16[16,8,128]{2,1,0:T(8,128)(2,1)S(1)}, u32[]{:S(2)}, u32[]{:S(2)}) %all-to-all-start) | async-done | bytes 32800 | tf_op jit(solution)/shard_map/all_to_all | solution.py:210
  21.7 1.6 %shard_map.74 = bf16[16,8,384]{2,1,0:T(8,128)(2,1)} custom-call(s32[8,4]{1,0:T(8,128)} %copy.9.ham_idx, s32[4,1]{1,0:T(4,128)} %copy.10.coef_idx, bf16[16,8,128]{2,1,0:T(8,128)(2,1)S(1)} %all-to-all-done.named, bf16[400,128]{1,0:T(8,128)(2,1)S(1)} %collective-permute-done.swapped, bf16[16,8,256]{2,1,0:T(8,128)(2,1)S(1)} %get-tuple-element.17.parts), custom_call_target="tpu_custom_call" | custom-call | tf_op jit(solution)/shard_map/pallas_call | solution.py:195
  23.3 8.3 %all-to-all-start.1 = ((bf16[16,8,384]{2,1,0:T(8,128)(2,1)}), bf16[16,8,384]{2,1,0:T(8,128)(2,1)S(1)}, u32[]{:S(2)}, u32[]{:S(2)}) async-start(bf16[16,8,384]{2,1,0:T(8,128)(2,1)} %shard_map.74), calls=%async_computation.1 | async-start | bytes 196608 | tf_op jit(solution)/shard_map/all_to_all | solution.py:227
  31.7 0.7 copy-done.2
  32.4 1.0 %collective-permute-start.1 = (bf16[2,128,128]{2,1,0:T(8,128)(2,1)S(1)}, bf16[2,128,128]{2,1,0:T(8,128)(2,1)S(1)}, u32[]{:S(2)}, u32[]{:S(2)}) collective-permute-start(bf16[2,128,128]{2,1,0:T(8,128)(2,1)S(1)} %get-tuple-element.28), channel_id=1, source_target_pairs={{0,8},{1,9},{2,10},{3,11},{4,12},{5,13},{6,14},{7,15},{8,0},{9,1},... | collective-permute-start | bytes 196616 | tf_op jit(solution)/shard_map/ppermute | solution.py:183
  33.4 5.6 %all-to-all-done.1.got = bf16[16,8,384]{2,1,0:T(8,128)(2,1)S(1)} async-done(((bf16[16,8,384]{2,1,0:T(8,128)(2,1)}), bf16[16,8,384]{2,1,0:T(8,128)(2,1)S(1)}, u32[]{:S(2)}, u32[]{:S(2)}) %all-to-all-start.1) | async-done | bytes 98336 | tf_op jit(solution)/shard_map/all_to_all | solution.py:227
  39.0 1.0 %shard_map.76 = bf16[16,16,256]{2,1,0:T(8,128)(2,1)} custom-call(bf16[16,8,384]{2,1,0:T(8,128)(2,1)S(1)} %all-to-all-done.1.got), custom_call_target="tpu_custom_call" | custom-call | tf_op jit(solution)/shard_map/pallas_call | solution.py:195
  40.1 3.5 %all-to-all-start.2 = ((bf16[16,16,256]{2,1,0:T(8,128)(2,1)}), bf16[16,16,256]{2,1,0:T(8,128)(2,1)S(1)}, u32[]{:S(2)}, u32[]{:S(2)}) async-start(bf16[16,16,256]{2,1,0:T(8,128)(2,1)} %shard_map.76), calls=%async_computation.2 | async-start | bytes 262144 | tf_op jit(solution)/shard_map/all_to_all | solution.py:234
  43.6 1.0 %collective-permute-start.4 = (bf16[2,2,128,128]{3,2,1,0:T(8,128)(2,1)S(1)}, bf16[2,2,128,128]{3,2,1,0:T(8,128)(2,1)S(1)}, u32[]{:S(2)}, u32[]{:S(2)}) collective-permute-start(bf16[2,2,128,128]{3,2,1,0:T(8,128)(2,1)S(1)} %pad_maximum_fusion.refs_8_), channel_id=1, source_target_pairs={{0,4},{1,5},{2,6},{3,7},{4,0},{5,1},{6,2},{7,3},{8,12},{9,13},{10,... | collective-permute-start | bytes 393224 | tf_op jit(solution)/shard_map/ppermute | solution.py:183
  44.6 1.8 %collective-permute-start.3 = (bf16[2,2,128,128]{3,2,1,0:T(8,128)(2,1)S(1)}, bf16[2,2,128,128]{3,2,1,0:T(8,128)(2,1)S(1)}, u32[]{:S(2)}, u32[]{:S(2)}) collective-permute-start(bf16[2,2,128,128]{3,2,1,0:T(8,128)(2,1)S(1)} %pad_maximum_fusion.refs_8_), channel_id=1, source_target_pairs={{0,6},{1,7},{2,0},{3,1},{4,2},{5,3},{6,4},{7,5},{8,14},{9,15},{10,... | collective-permute-start | bytes 393224 | tf_op jit(solution)/shard_map/ppermute | solution.py:183
  47.0 1.9 %shard_map.75 = bf16[16,4,64,128]{3,2,1,0:T(8,128)(2,1)} custom-call(s32[16,128]{1,0:T(8,128)} %bitcast.15, bf16[4,64,128]{2,1,0:T(8,128)(2,1)S(1)} %get-tuple-element.18.own, bf16[400,128]{1,0:T(8,128)(2,1)S(1)} %collective-permute-done.swapped), custom_call_target="tpu_custom_call" | custom-call | tf_op jit(solution)/shard_map/pallas_call | solution.py:195
  49.0 0.8 collective-permute-done.3.refs_10_
  49.8 3.2 %collective-permute-done.2.refs_9_ = bf16[2,2,128,128]{3,2,1,0:T(8,128)(2,1)S(1)} collective-permute-done((bf16[2,2,128,128]{3,2,1,0:T(8,128)(2,1)S(1)}, bf16[2,2,128,128]{3,2,1,0:T(8,128)(2,1)S(1)}, u32[]{:S(2)}, u32[]{:S(2)}) %collective-permute-start.2) | collective-permute-done | bytes 131104 | tf_op jit(solution)/shard_map/ppermute | solution.py:183
  53.1 7.3 %all-to-all-start.3 = ((bf16[16,4,64,128]{3,2,1,0:T(8,128)(2,1)}), bf16[16,4,64,128]{3,2,1,0:T(8,128)(2,1)S(1)}, u32[]{:S(2)}, u32[]{:S(2)}) async-start(bf16[16,4,64,128]{3,2,1,0:T(8,128)(2,1)} %shard_map.75), calls=%async_computation.3 | async-start | bytes 2097152 | tf_op jit(solution)/shard_map/all_to_all | solution.py:246
  60.5 1.2 %collective-permute-start.5 = (bf16[16,16,256]{2,1,0:T(8,128)(2,1)S(1)}, bf16[16,16,256]{2,1,0:T(8,128)(2,1)S(1)}, u32[]{:S(2)}, u32[]{:S(2)}) collective-permute-start(bf16[16,16,256]{2,1,0:T(8,128)(2,1)S(1)} %shard_map.77.refs_0_), channel_id=1, source_target_pairs={{0,8},{1,9},{2,10},{3,11},{4,12},{5,13},{6,14},{7,15},{8,0},{9,1},... | collective-permute-start | bytes 393224 | tf_op jit(solution)/shard_map/ppermute | solution.py:183
  61.7 1.0 %collective-permute-start.8 = (bf16[16,16,256]{2,1,0:T(8,128)(2,1)S(1)}, bf16[16,16,256]{2,1,0:T(8,128)(2,1)S(1)}, u32[]{:S(2)}, u32[]{:S(2)}) collective-permute-start(bf16[16,16,256]{2,1,0:T(8,128)(2,1)S(1)} %shard_map.77.refs_0_), channel_id=1, source_target_pairs={{0,6},{1,7},{2,0},{3,1},{4,2},{5,3},{6,4},{7,5},{8,14},{9,15},{10,... | collective-permute-start | bytes 393224 | tf_op jit(solution)/shard_map/ppermute | solution.py:183
  63.2 6.7 %collective-permute-done.5.refs_1_ = bf16[16,16,256]{2,1,0:T(8,128)(2,1)S(1)} collective-permute-done((bf16[16,16,256]{2,1,0:T(8,128)(2,1)S(1)}, bf16[16,16,256]{2,1,0:T(8,128)(2,1)S(1)}, u32[]{:S(2)}, u32[]{:S(2)}) %collective-permute-start.5) | collective-permute-done | bytes 131104 | tf_op jit(solution)/shard_map/ppermute | solution.py:183
  69.9 1.5 %collective-permute-start.7 = (bf16[16,16,256]{2,1,0:T(8,128)(2,1)S(1)}, bf16[16,16,256]{2,1,0:T(8,128)(2,1)S(1)}, u32[]{:S(2)}, u32[]{:S(2)}) collective-permute-start(bf16[16,16,256]{2,1,0:T(8,128)(2,1)S(1)} %collective-permute-done.5.refs_1_), channel_id=1, source_target_pairs={{0,2},{1,3},{2,4},{3,5},{4,6},{5,7},{6,0},{7,1},{8,10},{9,11},{10,... | collective-permute-start | bytes 393224 | tf_op jit(solution)/shard_map/ppermute | solution.py:183
  72.0 4.2 %match.1 = s32[256]{0:T(256)} custom-call(s32[128,4]{1,0:T(8,128)} %fusion.1.ham_names, s32[16,128]{1,0:T(8,128)} %bitcast.16), custom_call_target="tpu_custom_call" | custom-call | tf_op jit(solution)/shard_map/match/pallas_call | solution.py:254
  76.3 2.4 %collective-permute-done.7.refs_3_ = bf16[16,16,256]{2,1,0:T(8,128)(2,1)S(1)} collective-permute-done((bf16[16,16,256]{2,1,0:T(8,128)(2,1)S(1)}, bf16[16,16,256]{2,1,0:T(8,128)(2,1)S(1)}, u32[]{:S(2)}, u32[]{:S(2)}) %collective-permute-start.7) | collective-permute-done | bytes 131104 | tf_op jit(solution)/shard_map/ppermute | solution.py:183
  78.7 4.6 %all-to-all-done.3.coefs = bf16[16,4,64,128]{3,2,1,0:T(8,128)(2,1)S(1)} async-done(((bf16[16,4,64,128]{3,2,1,0:T(8,128)(2,1)}), bf16[16,4,64,128]{3,2,1,0:T(8,128)(2,1)S(1)}, u32[]{:S(2)}, u32[]{:S(2)}) %all-to-all-start.3) | async-done | bytes 1048608 | tf_op jit(solution)/shard_map/all_to_all | solution.py:246
  83.3 1.0 %copy-done = bf16[16,4,64,128]{3,2,1,0:T(8,128)(2,1)} copy-done((bf16[16,4,64,128]{3,2,1,0:T(8,128)(2,1)}, bf16[16,4,64,128]{3,2,1,0:T(8,128)(2,1)S(1)}, u32[]{:S(2)}) %copy-start) | copy-done | bytes 1048600
  84.3 1.2 %copy-done.1 = bf16[16,4,64,128]{3,2,1,0:T(8,128)(2,1)S(1)} copy-done((bf16[16,4,64,128]{3,2,1,0:T(8,128)(2,1)S(1)}, bf16[16,4,64,128]{3,2,1,0:T(8,128)(2,1)}, u32[]{:S(2)}) %copy-start.1) | copy-done | bytes 1048600
  85.5 4.2 %shard_map.78 = (f32[2,128,128]{2,1,0:T(8,128)S(1)}, bf16[2,128,128]{2,1,0:T(8,128)(2,1)S(1)}) custom-call(s32[256]{0:T(256)} %match.1, bf16[16,4,64,128]{3,2,1,0:T(8,128)(2,1)S(1)} %copy-done.1, bf16[16,16,256]{2,1,0:T(8,128)(2,1)S(1)} %shard_map.77.refs_0_, bf16[16,16,256]{2,1,0:T(8,128)(2,1)S(1)} %collective-permute-done.5.refs_1_, ...), custom_call_target="tpu_custom_call" | custom-call | tf_op jit(solution)/shard_map/pallas_call | solution.py:195
  89.7 5.2 %collective-permute-start.12 = (bf16[2,128,128]{2,1,0:T(8,128)(2,1)S(1)}, bf16[2,128,128]{2,1,0:T(8,128)(2,1)S(1)}, u32[]{:S(2)}, u32[]{:S(2)}) collective-permute-start(bf16[2,128,128]{2,1,0:T(8,128)(2,1)S(1)} %get-tuple-element.26), channel_id=1, source_target_pairs={{0,1},{1,0},{2,3},{3,2},{4,5},{5,4},{6,7},{7,6},{8,9},{9,8},{10,11... | collective-permute-start | bytes 196616 | tf_op jit(solution)/shard_map/ppermute | solution.py:276
  94.9 0.9 collective-permute-done.12
  95.8 0.6 fusion
  (30 shorter events, 3.5 us)
Async XLA Ops:
  3.6 18.1 %collective-permute-start = (bf16[400,128]{1,0:T(8,128)(2,1)S(1)}, bf16[400,128]{1,0:T(8,128)(2,1)S(1)}, u32[]{:S(2)}, u32[]{:S(2)}) collective-permute-start(bf16[400,128]{1,0:T(8,128)(2,1)S(1)} %get-tuple-element.16), channel_id=1, source_target_pairs={{0,1},{1,0},{2,3},{3,2},{4,5},{5,4},{6,7},{7,6},{8,9},{9,8},{10,11... | collective-permute-start | bytes 307208 | tf_op jit(solution)/shard_map/ppermute | solution.py:219
  7.6 0.7 copy-start.4
  9.0 5.5 %copy-start.3 = (s32[8,4]{0,1:T(4,128)S(1)}, s32[8,4]{0,1:T(4,128)}, u32[]{:S(2)}) copy-start(s32[8,4]{0,1:T(4,128)} %param.8) | copy-start | bytes 388
  9.0 12.8 %all-to-all-start = ((bf16[16,8,128]{2,1,0:T(8,128)(2,1)}), bf16[16,8,128]{2,1,0:T(8,128)(2,1)S(1)}, u32[]{:S(2)}, u32[]{:S(2)}) async-start(bf16[16,8,128]{2,1,0:T(8,128)(2,1)} %broadcast_in_dim.4), calls=%async_computation | async-start | bytes 65536 | tf_op jit(solution)/shard_map/all_to_all | solution.py:210
  23.3 15.7 %all-to-all-start.1 = ((bf16[16,8,384]{2,1,0:T(8,128)(2,1)}), bf16[16,8,384]{2,1,0:T(8,128)(2,1)S(1)}, u32[]{:S(2)}, u32[]{:S(2)}) async-start(bf16[16,8,384]{2,1,0:T(8,128)(2,1)} %shard_map.74), calls=%async_computation.1 | async-start | bytes 196608 | tf_op jit(solution)/shard_map/all_to_all | solution.py:227
  31.6 0.8 copy-start.2
  32.4 11.2 %collective-permute-start.1 = (bf16[2,128,128]{2,1,0:T(8,128)(2,1)S(1)}, bf16[2,128,128]{2,1,0:T(8,128)(2,1)S(1)}, u32[]{:S(2)}, u32[]{:S(2)}) collective-permute-start(bf16[2,128,128]{2,1,0:T(8,128)(2,1)S(1)} %get-tuple-element.28), channel_id=1, source_target_pairs={{0,8},{1,9},{2,10},{3,11},{4,12},{5,13},{6,14},{7,15},{8,0},{9,1},... | collective-permute-start | bytes 196616 | tf_op jit(solution)/shard_map/ppermute | solution.py:183
  40.1 13.0 %all-to-all-start.2 = ((bf16[16,16,256]{2,1,0:T(8,128)(2,1)}), bf16[16,16,256]{2,1,0:T(8,128)(2,1)S(1)}, u32[]{:S(2)}, u32[]{:S(2)}) async-start(bf16[16,16,256]{2,1,0:T(8,128)(2,1)} %shard_map.76), calls=%async_computation.2 | async-start | bytes 262144 | tf_op jit(solution)/shard_map/all_to_all | solution.py:234
  43.6 5.4 %collective-permute-start.4 = (bf16[2,2,128,128]{3,2,1,0:T(8,128)(2,1)S(1)}, bf16[2,2,128,128]{3,2,1,0:T(8,128)(2,1)S(1)}, u32[]{:S(2)}, u32[]{:S(2)}) collective-permute-start(bf16[2,2,128,128]{3,2,1,0:T(8,128)(2,1)S(1)} %pad_maximum_fusion.refs_8_), channel_id=1, source_target_pairs={{0,4},{1,5},{2,6},{3,7},{4,0},{5,1},{6,2},{7,3},{8,12},{9,13},{10,... | collective-permute-start | bytes 393224 | tf_op jit(solution)/shard_map/ppermute | solution.py:183
  44.6 5.2 %collective-permute-start.3 = (bf16[2,2,128,128]{3,2,1,0:T(8,128)(2,1)S(1)}, bf16[2,2,128,128]{3,2,1,0:T(8,128)(2,1)S(1)}, u32[]{:S(2)}, u32[]{:S(2)}) collective-permute-start(bf16[2,2,128,128]{3,2,1,0:T(8,128)(2,1)S(1)} %pad_maximum_fusion.refs_8_), channel_id=1, source_target_pairs={{0,6},{1,7},{2,0},{3,1},{4,2},{5,3},{6,4},{7,5},{8,14},{9,15},{10,... | collective-permute-start | bytes 393224 | tf_op jit(solution)/shard_map/ppermute | solution.py:183
  46.4 6.7 %collective-permute-start.2 = (bf16[2,2,128,128]{3,2,1,0:T(8,128)(2,1)S(1)}, bf16[2,2,128,128]{3,2,1,0:T(8,128)(2,1)S(1)}, u32[]{:S(2)}, u32[]{:S(2)}) collective-permute-start(bf16[2,2,128,128]{3,2,1,0:T(8,128)(2,1)S(1)} %pad_maximum_fusion.refs_8_), channel_id=1, source_target_pairs={{0,2},{1,3},{2,4},{3,5},{4,6},{5,7},{6,0},{7,1},{8,10},{9,11},{10,... | collective-permute-start | bytes 393224 | tf_op jit(solution)/shard_map/ppermute | solution.py:183
  53.1 30.2 %all-to-all-start.3 = ((bf16[16,4,64,128]{3,2,1,0:T(8,128)(2,1)}), bf16[16,4,64,128]{3,2,1,0:T(8,128)(2,1)S(1)}, u32[]{:S(2)}, u32[]{:S(2)}) async-start(bf16[16,4,64,128]{3,2,1,0:T(8,128)(2,1)} %shard_map.75), calls=%async_computation.3 | async-start | bytes 2097152 | tf_op jit(solution)/shard_map/all_to_all | solution.py:246
  60.5 9.4 %collective-permute-start.5 = (bf16[16,16,256]{2,1,0:T(8,128)(2,1)S(1)}, bf16[16,16,256]{2,1,0:T(8,128)(2,1)S(1)}, u32[]{:S(2)}, u32[]{:S(2)}) collective-permute-start(bf16[16,16,256]{2,1,0:T(8,128)(2,1)S(1)} %shard_map.77.refs_0_), channel_id=1, source_target_pairs={{0,8},{1,9},{2,10},{3,11},{4,12},{5,13},{6,14},{7,15},{8,0},{9,1},... | collective-permute-start | bytes 393224 | tf_op jit(solution)/shard_map/ppermute | solution.py:183
  61.7 8.2 %collective-permute-start.10 = (bf16[16,16,256]{2,1,0:T(8,128)(2,1)S(1)}, bf16[16,16,256]{2,1,0:T(8,128)(2,1)S(1)}, u32[]{:S(2)}, u32[]{:S(2)}) collective-permute-start(bf16[16,16,256]{2,1,0:T(8,128)(2,1)S(1)} %shard_map.77.refs_0_), channel_id=1, source_target_pairs={{0,4},{1,5},{2,6},{3,7},{4,0},{5,1},{6,2},{7,3},{8,12},{9,13},{10,... | collective-permute-start | bytes 393224 | tf_op jit(solution)/shard_map/ppermute | solution.py:183
  61.7 14.5 %collective-permute-start.8 = (bf16[16,16,256]{2,1,0:T(8,128)(2,1)S(1)}, bf16[16,16,256]{2,1,0:T(8,128)(2,1)S(1)}, u32[]{:S(2)}, u32[]{:S(2)}) collective-permute-start(bf16[16,16,256]{2,1,0:T(8,128)(2,1)S(1)} %shard_map.77.refs_0_), channel_id=1, source_target_pairs={{0,6},{1,7},{2,0},{3,1},{4,2},{5,3},{6,4},{7,5},{8,14},{9,15},{10,... | collective-permute-start | bytes 393224 | tf_op jit(solution)/shard_map/ppermute | solution.py:183
  62.7 13.5 %collective-permute-start.6 = (bf16[16,16,256]{2,1,0:T(8,128)(2,1)S(1)}, bf16[16,16,256]{2,1,0:T(8,128)(2,1)S(1)}, u32[]{:S(2)}, u32[]{:S(2)}) collective-permute-start(bf16[16,16,256]{2,1,0:T(8,128)(2,1)S(1)} %shard_map.77.refs_0_), channel_id=1, source_target_pairs={{0,2},{1,3},{2,4},{3,5},{4,6},{5,7},{6,0},{7,1},{8,10},{9,11},{10,... | collective-permute-start | bytes 393224 | tf_op jit(solution)/shard_map/ppermute | solution.py:183
  69.9 6.3 %collective-permute-start.11 = (bf16[16,16,256]{2,1,0:T(8,128)(2,1)S(1)}, bf16[16,16,256]{2,1,0:T(8,128)(2,1)S(1)}, u32[]{:S(2)}, u32[]{:S(2)}) collective-permute-start(bf16[16,16,256]{2,1,0:T(8,128)(2,1)S(1)} %collective-permute-done.5.refs_1_), channel_id=1, source_target_pairs={{0,4},{1,5},{2,6},{3,7},{4,0},{5,1},{6,2},{7,3},{8,12},{9,13},{10,... | collective-permute-start | bytes 393224 | tf_op jit(solution)/shard_map/ppermute | solution.py:183
  69.9 6.3 %collective-permute-start.9 = (bf16[16,16,256]{2,1,0:T(8,128)(2,1)S(1)}, bf16[16,16,256]{2,1,0:T(8,128)(2,1)S(1)}, u32[]{:S(2)}, u32[]{:S(2)}) collective-permute-start(bf16[16,16,256]{2,1,0:T(8,128)(2,1)S(1)} %collective-permute-done.5.refs_1_), channel_id=1, source_target_pairs={{0,6},{1,7},{2,0},{3,1},{4,2},{5,3},{6,4},{7,5},{8,14},{9,15},{10,... | collective-permute-start | bytes 393224 | tf_op jit(solution)/shard_map/ppermute | solution.py:183
  69.9 8.7 %collective-permute-start.7 = (bf16[16,16,256]{2,1,0:T(8,128)(2,1)S(1)}, bf16[16,16,256]{2,1,0:T(8,128)(2,1)S(1)}, u32[]{:S(2)}, u32[]{:S(2)}) collective-permute-start(bf16[16,16,256]{2,1,0:T(8,128)(2,1)S(1)} %collective-permute-done.5.refs_1_), channel_id=1, source_target_pairs={{0,2},{1,3},{2,4},{3,5},{4,6},{5,7},{6,0},{7,1},{8,10},{9,11},{10,... | collective-permute-start | bytes 393224 | tf_op jit(solution)/shard_map/ppermute | solution.py:183
  83.3 1.0 %copy-start = (bf16[16,4,64,128]{3,2,1,0:T(8,128)(2,1)}, bf16[16,4,64,128]{3,2,1,0:T(8,128)(2,1)S(1)}, u32[]{:S(2)}) copy-start(bf16[16,4,64,128]{3,2,1,0:T(8,128)(2,1)S(1)} %all-to-all-done.3.coefs) | copy-start | bytes 3145732
  84.3 1.2 %copy-start.1 = (bf16[16,4,64,128]{3,2,1,0:T(8,128)(2,1)S(1)}, bf16[16,4,64,128]{3,2,1,0:T(8,128)(2,1)}, u32[]{:S(2)}) copy-start(bf16[16,4,64,128]{3,2,1,0:T(8,128)(2,1)} %copy-done) | copy-start | bytes 3145732
  89.7 6.1 %collective-permute-start.12 = (bf16[2,128,128]{2,1,0:T(8,128)(2,1)S(1)}, bf16[2,128,128]{2,1,0:T(8,128)(2,1)S(1)}, u32[]{:S(2)}, u32[]{:S(2)}) collective-permute-start(bf16[2,128,128]{2,1,0:T(8,128)(2,1)S(1)} %get-tuple-element.26), channel_id=1, source_target_pairs={{0,1},{1,0},{2,3},{3,2},{4,5},{5,4},{6,7},{7,6},{8,9},{9,8},{10,11... | collective-permute-start | bytes 196616 | tf_op jit(solution)/shard_map/ppermute | solution.py:276
where the time goes:
time: 97.2 us; the launch traced here: 96.5 us
  starting transfers between devices  41 us (42%)
  waiting for transfers between devices  31.1 us (32%)
  Pallas kernels  15.4 us (16%)
  local copies, waits for them, and re-layouts  6.25 us (6%)
  other arithmetic  1.99 us (2%)
    ppermute x11, waiting for transfers between devices, shift(): return lax.ppermute(value, 'col', pairs)  13.3 us
    pallas_call x6, Pallas kernels, run(): pl.pallas_call(kernel, out_shape=[pltpu.VMEM(shape, kind) for shape, kind...  11.2 us
    all_to_all x1, starting transfers between devices, body(): got = lax.all_to_all(stamped, 'row', 0, 0)  8.32 us
    ppermute x11, starting transfers between devices, shift(): return lax.ppermute(value, 'col', pairs)  7.89 us
    all_to_all x1, starting transfers between devices, body(): coefs = lax.all_to_all(wanted, 'row', 0, 0)  7.26 us
    all_to_all x1, waiting for transfers between devices, body(): named = lax.all_to_all(names, 'col', 0, 0)  6.63 us
    all_to_all x1, waiting for transfers between devices, body(): got = lax.all_to_all(stamped, 'row', 0, 0)  5.64 us
    unnamed x12, local copies, waits for them, and re-layouts  5.62 us
  transfers between devices with their start and end apart: 17, of which 9 were waited for; matrix products, arithmetic and copies ran while one was open for 3% of the time, Pallas kernels for 8%

commit v1 on v0

--- a/solution.py
+++ b/solution.py
@@ -1,3 +1,5 @@
+import functools
+
 import jax
 import jax.numpy as jnp
 from jax import lax
@@ -26,6 +28,12 @@
 
 def dot(a, b):
     return jnp.dot(a, b, preferred_element_type=F32)
+
+
+def name_kernel(slab_idx, pattern, send):
+    lane = iota((8, 128), 1)
+    line = jnp.where(lane == 0, slab_idx[0, 0], jnp.where(lane == 1, pattern[0, 0], pattern[0, 1]))
+    send[...] = jnp.broadcast_to(line.astype(F32).astype(BF)[None], send.shape)
 
 
 def split_kernel(coef_idx, ham, coef, slab, send, own, swap, part, turned, sem):
@@ -104,7 +112,7 @@
         for i in range(4):
             at = 2 * chip + i // 2
             j = tables[r, 32 + 2 * at + i % 2] - 4 * at
-            send[r, i] = both[i // 2, j]
+            send[r, 64 * i : 64 * i + 64] = both[i // 2, j]
 
 
 def match_kernel(ham_names, tables, out, slots):
@@ -112,11 +120,11 @@
     chip, core = col // 2, col % 2
 
     def clear(q, _):
-        for i in range(4):
-            slots[i * 128 + q] = -1
+        for i in range(64):
+            slots[q * 64 + i] = -1
         return 0
 
-    lax.fori_loop(0, 128, clear, 0)
+    lax.fori_loop(0, 8, clear, 0)
     for i in range(4):
         at = 2 * chip + i // 2
         j = tables[row, 32 + 2 * at + i % 2] - 4 * at
@@ -124,53 +132,44 @@
         for m in range(16):
             slots[i * 128 + tables[m, base]] = m
 
-    def one(m, _):
+    for m in range(16):
         p = tables[row, 16 + m]
         for k in range(4):
             q = ham_names[p, k]
             for i in range(4):
                 out[m * 16 + k * 4 + i] = jnp.where(q >= 0, slots[i * 128 + jnp.maximum(q, 0)], -1)
-        return 0
-
-    lax.fori_loop(0, 16, one, 0)
-
-
-def product_kernel(match, coefs, *refs):
-    hams, slabs, (own, send), (ham, slab, image, chosen, sems) = refs[:8], refs[8:12], refs[12:14], refs[14:]
+
+
+def gather_kernel(*refs):
+    hams, slabs, (ham, slab) = refs[:8], refs[8:10], refs[10:]
     col = lax.axis_index("col")
     chip, core = col // 2, col % 2
     x, y = chip // 4, chip % 4
-    copies = []
     for t, (dx, dy) in enumerate(PLACES):
         s = ((x + dx) % 2) * 4 + (y - dy + 4) % 4
-        at = pl.ds(pl.multiple_of(s * 16, 16), 16)
-        copies.append(pltpu.make_async_copy(hams[t], ham.at[:, at, :], sems.at[t]))
-        if t % 2 == 0:
-            for h in range(2):
-                s = ((x + h) % 2) * 4 + (y - dy + 4) % 4
-                copies.append(pltpu.make_async_copy(slabs[t // 2].at[h], slab.at[s], sems.at[8 + t + h]))
-    for copy in copies:
-        copy.start()
-    for copy in copies:
-        copy.wait()
-
-    total = jnp.zeros((128, 512), F32)
-    for s in range(8):
+        ham[:, pl.ds(pl.multiple_of(s * 16, 16), 16), :] = hams[t][...]
         for h in range(2):
-            m = 2 * s + (core + h) % 2
-            for k in range(4):
-                for i in range(4):
-                    slot = match[m * 16 + k * 4 + i]
-                    found = coefs[jnp.maximum(slot, 0), i]
-                    chosen[h, k * 64 : k * 64 + 64, i * 128 : i * 128 + 128] = jnp.where(slot >= 0, found, jnp.zeros_like(found))
-            image[s, h * 128 : h * 128 + 128, :] = dot(ham[m], chosen[h]).astype(BF)
-    for s in range(8):
-        for h in range(2):
-            total = total + dot(slab[s, h], image[s, h * 128 : h * 128 + 128, :])
+            slab[2 * s + (core + h) % 2] = slabs[dx][t // 2, h]
+
+
+def product_kernel(mine, match, coefs, ham, slab, out, image, chosen):
+    core = lax.axis_index("col") % 2
+    pair = core if mine else 1 - core
+    total = jnp.zeros((128, 256), F32)
+    for m in range(16):
+        for k in range(4):
+            for e in range(2):
+                slot = match[m * 16 + k * 4 + 2 * pair + e]
+                at = pl.ds(pl.multiple_of(128 * pair + 64 * e, 64), 64)
+                found = coefs[jnp.maximum(slot, 0), at]
+                chosen[m % 4, k * 64 : k * 64 + 64, e * 128 : e * 128 + 128] = jnp.where(
+                    slot >= 0, found, jnp.zeros_like(found)
+                )
+        image[m] = dot(ham[m], chosen[m % 4]).astype(BF)
+    for m in range(16):
+        total = total + dot(slab[m], image[m])
     for e in range(2):
-        low, high = total[:, e * 128 : e * 128 + 128], total[:, 256 + e * 128 : 384 + e * 128]
-        own[e] = jnp.where(core == 0, low, high)
-        send[e] = jnp.where(core == 0, high, low).astype(BF)
+        out[e] = total[:, e * 128 : e * 128 + 128].astype(out.dtype)
 
 
 def shift(value, dx, dy):
@@ -187,7 +186,7 @@
     return pltpu.with_memory_space_constraint(value, pltpu.VMEM)
 
 
-def run(kernel, outs, specs, args, scratch=()):
+def run(kernel, outs, specs, args, scratch=(), limit=None):
     args = [near(v) if spec == "near" else v for spec, v in zip(specs, args)]
     specs = [VMEM if spec == "near" else spec for spec in specs]
     single = not isinstance(outs, list)
@@ -198,6 +197,7 @@
         in_specs=specs,
         out_specs=[VMEM] * len(outs),
         scratch_shapes=scratch,
+        compiler_params=pltpu.CompilerParams(vmem_limit_bytes=limit),
     )(*args)
     return result[0] if single else result
 
@@ -205,8 +205,7 @@
 def body(ham_blocks, ham_index, coef_blocks, coef_index, slab_blocks, slab_index, pattern_index):
     cores = [(i, i ^ 1) for i in range(COLS)]
 
-    names = jnp.concatenate([slab_index, pattern_index], axis=1).astype(BF)
-    names = jnp.broadcast_to(jnp.pad(names, ((0, 7), (0, 125)))[None], (COLS, 8, 128))
+    names = run(name_kernel, ((COLS, 8, 128), BF), [SMEM, SMEM], [slab_index, pattern_index])
     named = lax.all_to_all(names, "col", 0, 0)
 
     parts, half, swap = run(
@@ -227,8 +226,9 @@
     got = lax.all_to_all(stamped, "row", 0, 0)
 
     pair = jnp.stack([slab_blocks[0, 0], swapped[256:384]]).reshape(2, 128, 128)
-    quad = jnp.stack([pair, shift(pair, 1, 0)])
-    quads = [quad] + [shift(quad, 0, d) for d in (1, 3, 2)]
+    line = [pair] + [shift(pair, 0, d) for d in (1, 3, 2)]
+    line = jnp.stack(line)
+    slabs = [line, shift(line, 1, 0)]
 
     picked = run(pick_kernel, ((16, 16, 256), BF), ["near"], [got])
     picks = lax.all_to_all(picked, "row", 0, 0)
@@ -237,12 +237,12 @@
     ham_names = got[:, :, 256:260].reshape(128, 4).astype(I32)
     wanted = run(
         choose_kernel,
-        ((16, 4, 64, 128), BF),
+        ((16, 256, 128), BF),
         [SMEM, "near", "near"],
         [numbers, half, swapped],
         [pltpu.VMEM((2, 4, 64, 128), BF)],
     )
-    wanted, picks, *quads = lax.optimization_barrier((wanted, picks, *quads))
+    wanted, picks = lax.optimization_barrier((wanted, picks))
     coefs = lax.all_to_all(wanted, "row", 0, 0)
 
     piece = run(pack_kernel, ((16, 16, 256), BF), ["near"], [picks])
@@ -253,27 +253,35 @@
 
     match = pl.pallas_call(
         match_kernel,
-        out_shape=jax.ShapeDtypeStruct((256,), I32),
+        out_shape=pltpu.SMEM((256,), I32),
         in_specs=[SMEM] * 2,
         out_specs=SMEM,
         scratch_shapes=[pltpu.SMEM((512,), I32)],
         name="match",
     )(ham_names, numbers)
-
-    mine, other = run(
-        product_kernel,
-        [((2, 128, 128), F32), ((2, 128, 128), BF)],
-        [SMEM] + ["near"] * 13,
-        [match, coefs, *hams, *quads],
-        [
-            pltpu.VMEM((16, 128, 256), BF),
-            pltpu.VMEM((8, 2, 128, 128), BF),
-            pltpu.VMEM((8, 256, 512), BF),
-            pltpu.VMEM((2, 256, 512), BF),
-            pltpu.SemaphoreType.DMA((16,)),
-        ],
-    )
+    match = pltpu.with_memory_space_constraint(match, pltpu.SMEM)
+
+    ham, slab = run(
+        gather_kernel,
+        [((16, 128, 256), BF), ((16, 128, 128), BF)],
+        ["near"] * 10,
+        [*hams, *slabs],
+        limit=24 << 20,
+    )
+
+    def product(mine, kind):
+        return run(
+            functools.partial(product_kernel, mine),
+            ((2, 128, 128), kind),
+            [SMEM] + ["near"] * 3,
+            [match, coefs, ham, slab],
+            [pltpu.VMEM((16, 128, 256), BF), pltpu.VMEM((4, 256, 256), BF)],
+            24 << 20,
+        )
+
+    other = product(False, BF)
     theirs = lax.ppermute(other, "col", cores)
+    mine = product(True, F32)
     return (mine + theirs.astype(F32)).astype(BF)[None]
 
 

time: 97.2 us -> 99.7 us (1.026)
  blocking collectives: 0 us -> 15.5 us
  starting transfers between devices: 41 us -> 31.2 us
  waiting for transfers between devices: 31.1 us -> 26 us
  local copies, waits for them, and re-layouts: 6.25 us -> 10.5 us
  Pallas kernels: 15.4 us -> 13 us
    all_to_all x0 -> x1, blocking collectives: none -> 15.5 us  [body(): got = lax.all_to_all(stamped, 'row', 0, 0)]
    all_to_all x1 -> x0, starting transfers between devices: 8.32 us -> none  [body(): got = lax.all_to_all(stamped, 'row', 0, 0)]
    all_to_all x1 -> x0, waiting for transfers between devices: 5.64 us -> none  [body(): got = lax.all_to_all(stamped, 'row', 0, 0)]
    all_to_all x1, waiting for transfers between devices: 0.01 us -> 4.98 us  [body(): picks = lax.all_to_all(picked, 'row', 0, 0)]
    unnamed x12 -> x26, local copies, waits for them, and re-layouts: 5.62 us -> 10.5 us
    all_to_all x1, waiting for transfers between devices: 4.58 us -> 0.01 us  [body(): coefs = lax.all_to_all(wanted, 'row', 0, 0)]
    ppermute x11, starting transfers between devices: 7.89 us -> 11.7 us  [shift(): return lax.ppermute(value, 'col', pairs)]
    all_to_all x1, starting transfers between devices: 7.26 us -> 3.65 us  [body(): coefs = lax.all_to_all(wanted, 'row', 0, 0)]
  transfers between devices with their start and end apart: 17 -> 16, of which waited for: 9 -> 7; matrix products, arithmetic and copies ran while one was open for 3% -> 2% of each run, Pallas kernels for 8% -> 8%
where the time goes in v1:
time: 99.7 us; the launch traced here: 99 us
  starting transfers between devices  31.2 us (31%)
  waiting for transfers between devices  26 us (26%)
  blocking collectives  15.5 us (16%)
  Pallas kernels  13 us (13%)
  local copies, waits for them, and re-layouts  10.5 us (11%)
  other arithmetic  1.93 us (2%)
    all_to_all x1, blocking collectives, body(): got = lax.all_to_all(stamped, 'row', 0, 0)  15.5 us
    ppermute x11, waiting for transfers between devices, shift(): return lax.ppermute(value, 'col', pairs)  14.3 us
    ppermute x11, starting transfers between devices, shift(): return lax.ppermute(value, 'col', pairs)  11.7 us
    unnamed x26, local copies, waits for them, and re-layouts  10.5 us
    pallas_call x9, Pallas kernels, run(): pl.pallas_call(kernel, out_shape=[pltpu.VMEM(shape, kind) for shape, kind...  10.2 us
    all_to_all x1, waiting for transfers between devices, body(): named = lax.all_to_all(names, 'col', 0, 0)  6.63 us
    all_to_all x1, starting transfers between devices, body(): named = lax.all_to_all(names, 'col', 0, 0)  5.48 us
    all_to_all x1, waiting for transfers between devices, body(): picks = lax.all_to_all(picked, 'row', 0, 0)  4.98 us
  transfers between devices with their start and end apart: 16, of which 7 were waited for; matrix products, arithmetic and copies ran while one was open for 2% of the time, Pallas kernels for 8%

profile of v1, /device:TPU:1, one launch (start us, length us, event | category | flops | bytes accessed | tf_op | source)
XLA Modules:
  0.0 99.0 jit_solution(10978926360339284699)
XLA Ops:
  0.0 1.3 %copy.10.coef_idx = s32[4,1]{1,0:T(4,128)} copy(s32[4,1]{0,1:T(1,128)} %param.10) | data formatting | bytes 32 | tf_op args[3]
  1.3 2.3 %shard_map.74 = (bf16[16,8,256]{2,1,0:T(8,128)(2,1)S(1)}, bf16[4,64,128]{2,1,0:T(8,128)(2,1)S(1)}, bf16[400,128]{1,0:T(8,128)(2,1)S(1)}) custom-call(s32[4,1]{1,0:T(4,128)} %copy.10.coef_idx, bf16[8,4,128,128]{3,2,1,0:T(8,128)(2,1)} %ham.1, bf16[4,1,128,128]{3,2,1,0:T(8,128)(2,1)} %coef.1, bf16[1,1,128,128]{3,2,1,0:T(8,128)(2,1)} %slab.1), custom_call_target="tpu_custom_call" | custom-call | tf_op jit(solution)/shard_map/pallas_call | solution.py:194
  3.6 3.3 %collective-permute-start = (bf16[400,128]{1,0:T(8,128)(2,1)S(1)}, bf16[400,128]{1,0:T(8,128)(2,1)S(1)}, u32[]{:S(2)}, u32[]{:S(2)}) collective-permute-start(bf16[400,128]{1,0:T(8,128)(2,1)S(1)} %get-tuple-element.12), channel_id=1, source_target_pairs={{0,1},{1,0},{2,3},{3,2},{4,5},{5,4},{6,7},{7,6},{8,9},{9,8},{10,11... | collective-permute-start | bytes 307208 | tf_op jit(solution)/shard_map/ppermute | solution.py:218
  7.6 1.3 %shard_map.73 = bf16[16,8,128]{2,1,0:T(8,128)(2,1)} custom-call(s32[1,1]{1,0:T(1,128)S(6)} %copy.11.slab_idx, s32[1,2]{1,0:T(1,128)} %pattern.1), custom_call_target="tpu_custom_call" | custom-call | tf_op jit(solution)/shard_map/pallas_call | solution.py:194
  8.9 5.5 %all-to-all-start = ((bf16[16,8,128]{2,1,0:T(8,128)(2,1)}), bf16[16,8,128]{2,1,0:T(8,128)(2,1)S(1)}, u32[]{:S(2)}, u32[]{:S(2)}) async-start(bf16[16,8,128]{2,1,0:T(8,128)(2,1)} %shard_map.73), calls=%async_computation | async-start | bytes 65536 | tf_op jit(solution)/shard_map/all_to_all | solution.py:209
  15.0 6.6 %all-to-all-done.named = bf16[16,8,128]{2,1,0:T(8,128)(2,1)S(1)} async-done(((bf16[16,8,128]{2,1,0:T(8,128)(2,1)}), bf16[16,8,128]{2,1,0:T(8,128)(2,1)S(1)}, u32[]{:S(2)}, u32[]{:S(2)}) %all-to-all-start) | async-done | bytes 32800 | tf_op jit(solution)/shard_map/all_to_all | solution.py:209
  21.6 0.9 shard_map.75
  22.6 15.5 %all_to_all.20.got = bf16[16,8,384]{2,1,0:T(8,128)(2,1)S(1)} all-to-all(bf16[16,8,384]{2,1,0:T(8,128)(2,1)S(1)} %shard_map.75), channel_id=1, replica_groups=mesh['row'=16,'col'=16] {'row'}, dimensions={0} | all-to-all | bytes 196608 | tf_op jit(solution)/shard_map/all_to_all | solution.py:226
  38.1 1.0 %shard_map.77 = bf16[16,16,256]{2,1,0:T(8,128)(2,1)} custom-call(bf16[16,8,384]{2,1,0:T(8,128)(2,1)S(1)} %all_to_all.20.got), custom_call_target="tpu_custom_call" | custom-call | tf_op jit(solution)/shard_map/pallas_call | solution.py:194
  39.1 3.5 %all-to-all-start.2 = ((bf16[16,16,256]{2,1,0:T(8,128)(2,1)}), bf16[16,16,256]{2,1,0:T(8,128)(2,1)S(1)}, u32[]{:S(2)}, u32[]{:S(2)}) async-start(bf16[16,16,256]{2,1,0:T(8,128)(2,1)} %shard_map.77), calls=%async_computation.2 | async-start | bytes 262144 | tf_op jit(solution)/shard_map/all_to_all | solution.py:234
  43.2 1.9 %shard_map.76 = bf16[16,256,128]{2,1,0:T(8,128)(2,1)} custom-call(s32[16,128]{1,0:T(8,128)} %bitcast.17, bf16[4,64,128]{2,1,0:T(8,128)(2,1)S(1)} %get-tuple-element.14.own, bf16[400,128]{1,0:T(8,128)(2,1)S(1)} %collective-permute-done.swapped), custom_call_target="tpu_custom_call" | custom-call | tf_op jit(solution)/shard_map/pallas_call | solution.py:194
  45.1 5.0 %all-to-all-done.2.got = bf16[16,16,256]{2,1,0:T(8,128)(2,1)S(1)} async-done(((bf16[16,16,256]{2,1,0:T(8,128)(2,1)}), bf16[16,16,256]{2,1,0:T(8,128)(2,1)S(1)}, u32[]{:S(2)}, u32[]{:S(2)}) %all-to-all-start.2) | async-done | bytes 131104 | tf_op jit(solution)/shard_map/all_to_all | solution.py:234
  50.1 3.7 %all-to-all-start.3 = ((bf16[16,256,128]{2,1,0:T(8,128)(2,1)}), bf16[16,256,128]{2,1,0:T(8,128)(2,1)S(1)}, u32[]{:S(2)}, u32[]{:S(2)}) async-start(bf16[16,256,128]{2,1,0:T(8,128)(2,1)} %shard_map.76), calls=%async_computation.3 | async-start | bytes 2097152 | tf_op jit(solution)/shard_map/all_to_all | solution.py:246
  54.5 1.0 %collective-permute-start.9 = (bf16[2,128,128]{2,1,0:T(8,128)(2,1)S(1)}, bf16[2,128,128]{2,1,0:T(8,128)(2,1)S(1)}, u32[]{:S(2)}, u32[]{:S(2)}) collective-permute-start(bf16[2,128,128]{2,1,0:T(8,128)(2,1)S(1)} %get-tuple-element.20), channel_id=1, source_target_pairs={{0,6},{1,7},{2,0},{3,1},{4,2},{5,3},{6,4},{7,5},{8,14},{9,15},{10,... | collective-permute-start | bytes 196616 | tf_op jit(solution)/shard_map/ppermute | solution.py:182
  56.1 0.9 collective-permute-start.10
  57.7 2.2 %collective-permute-done.8 = bf16[2,128,128]{2,1,0:T(8,128)(2,1)S(1)} collective-permute-done((bf16[2,128,128]{2,1,0:T(8,128)(2,1)S(1)}, bf16[2,128,128]{2,1,0:T(8,128)(2,1)S(1)}, u32[]{:S(2)}, u32[]{:S(2)}) %collective-permute-start.8) | collective-permute-done | bytes 65568 | tf_op jit(solution)/shard_map/ppermute | solution.py:182
  60.7 1.0 %collective-permute-start.11 = (bf16[4,2,128,128]{3,2,1,0:T(8,128)(2,1)S(1)}, bf16[4,2,128,128]{3,2,1,0:T(8,128)(2,1)S(1)}, u32[]{:S(2)}, u32[]{:S(2)}) collective-permute-start(bf16[4,2,128,128]{3,2,1,0:T(8,128)(2,1)S(1)} %pad_maximum_fusion.refs_8_), channel_id=1, source_target_pairs={{0,8},{1,9},{2,10},{3,11},{4,12},{5,13},{6,14},{7,15},{8,0},{9,1},... | collective-permute-start | bytes 786440 | tf_op jit(solution)/shard_map/ppermute | solution.py:182
  61.9 2.1 %collective-permute-start.1 = (bf16[16,16,256]{2,1,0:T(8,128)(2,1)S(1)}, bf16[16,16,256]{2,1,0:T(8,128)(2,1)S(1)}, u32[]{:S(2)}, u32[]{:S(2)}) collective-permute-start(bf16[16,16,256]{2,1,0:T(8,128)(2,1)S(1)} %shard_map.78.refs_0_), channel_id=1, source_target_pairs={{0,8},{1,9},{2,10},{3,11},{4,12},{5,13},{6,14},{7,15},{8,0},{9,1},... | collective-permute-start | bytes 393224 | tf_op jit(solution)/shard_map/ppermute | solution.py:182
  64.1 0.9 collective-permute-start.6
  65.0 2.1 %collective-permute-start.4 = (bf16[16,16,256]{2,1,0:T(8,128)(2,1)S(1)}, bf16[16,16,256]{2,1,0:T(8,128)(2,1)S(1)}, u32[]{:S(2)}, u32[]{:S(2)}) collective-permute-start(bf16[16,16,256]{2,1,0:T(8,128)(2,1)S(1)} %shard_map.78.refs_0_), channel_id=1, source_target_pairs={{0,6},{1,7},{2,0},{3,1},{4,2},{5,3},{6,4},{7,5},{8,14},{9,15},{10,... | collective-permute-start | bytes 393224 | tf_op jit(solution)/shard_map/ppermute | solution.py:182
  67.1 10.2 %collective-permute-done.1.refs_1_ = bf16[16,16,256]{2,1,0:T(8,128)(2,1)S(1)} collective-permute-done((bf16[16,16,256]{2,1,0:T(8,128)(2,1)S(1)}, bf16[16,16,256]{2,1,0:T(8,128)(2,1)S(1)}, u32[]{:S(2)}, u32[]{:S(2)}) %collective-permute-start.1) | collective-permute-done | bytes 131104 | tf_op jit(solution)/shard_map/ppermute | solution.py:182
  77.3 0.9 collective-permute-start.7
  78.2 2.2 %collective-permute-start.5 = (bf16[16,16,256]{2,1,0:T(8,128)(2,1)S(1)}, bf16[16,16,256]{2,1,0:T(8,128)(2,1)S(1)}, u32[]{:S(2)}, u32[]{:S(2)}) collective-permute-start(bf16[16,16,256]{2,1,0:T(8,128)(2,1)S(1)} %collective-permute-done.1.refs_1_), channel_id=1, source_target_pairs={{0,6},{1,7},{2,0},{3,1},{4,2},{5,3},{6,4},{7,5},{8,14},{9,15},{10,... | collective-permute-start | bytes 393224 | tf_op jit(solution)/shard_map/ppermute | solution.py:182
  81.0 2.8 %match.1 = s32[256]{0:T(256)S(4)} custom-call(s32[128,4]{1,0:T(8,128)} %fusion.1.ham_names, s32[16,128]{1,0:T(8,128)} %bitcast.18), custom_call_target="tpu_custom_call" | custom-call | tf_op jit(solution)/shard_map/match/pallas_call | solution.py:254
  87.5 0.9 copy-done.1
  88.4 0.9 copy-done.3
  89.3 0.9 copy-done.5
  90.2 0.9 copy-done.7
  91.1 0.9 copy-done.9
  92.2 1.3 %shard_map.81 = bf16[2,128,128]{2,1,0:T(8,128)(2,1)S(1)} custom-call(s32[256]{0:T(256)S(4)} %match.1, bf16[16,256,128]{2,1,0:T(8,128)(2,1)S(1)} %all-to-all-done.3.coefs, bf16[16,128,256]{2,1,0:T(8,128)(2,1)S(1)} %get-tuple-element.17.ham, bf16[16,128,128]{2,1,0:T(8,128)(2,1)S(1)} %get-tuple-element.18.slab), custom_call_target="tpu_custom_call" | custom-call | tf_op jit(solution)/shard_map/pallas_call | solution.py:194
  93.4 3.6 %collective-permute-start.12 = (bf16[2,128,128]{2,1,0:T(8,128)(2,1)S(1)}, bf16[2,128,128]{2,1,0:T(8,128)(2,1)S(1)}, u32[]{:S(2)}, u32[]{:S(2)}) collective-permute-start(bf16[2,128,128]{2,1,0:T(8,128)(2,1)S(1)} %shard_map.81), channel_id=1, source_target_pairs={{0,1},{1,0},{2,3},{3,2},{4,5},{5,4},{6,7},{7,6},{8,9},{9,8},{10,11... | collective-permute-start | bytes 196616 | tf_op jit(solution)/shard_map/ppermute | solution.py:283
  97.0 1.2 %shard_map.80 = f32[2,128,128]{2,1,0:T(8,128)S(1)} custom-call(s32[256]{0:T(256)S(4)} %match.1, bf16[16,256,128]{2,1,0:T(8,128)(2,1)S(1)} %all-to-all-done.3.coefs, bf16[16,128,256]{2,1,0:T(8,128)(2,1)S(1)} %get-tuple-element.17.ham, bf16[16,128,128]{2,1,0:T(8,128)(2,1)S(1)} %get-tuple-element.18.slab), custom_call_target="tpu_custom_call" | custom-call | tf_op jit(solution)/shard_map/pallas_call | solution.py:194
  (43 shorter events, 9.4 us)
Async XLA Ops:
  3.6 18.0 %collective-permute-start = (bf16[400,128]{1,0:T(8,128)(2,1)S(1)}, bf16[400,128]{1,0:T(8,128)(2,1)S(1)}, u32[]{:S(2)}, u32[]{:S(2)}) collective-permute-start(bf16[400,128]{1,0:T(8,128)(2,1)S(1)} %get-tuple-element.12), channel_id=1, source_target_pairs={{0,1},{1,0},{2,3},{3,2},{4,5},{5,4},{6,7},{7,6},{8,9},{9,8},{10,11... | collective-permute-start | bytes 307208 | tf_op jit(solution)/shard_map/ppermute | solution.py:218
  8.9 5.5 %copy-start.11 = (s32[8,4]{0,1:T(4,128)S(1)}, s32[8,4]{0,1:T(4,128)}, u32[]{:S(2)}) copy-start(s32[8,4]{0,1:T(4,128)} %param.8) | copy-start | bytes 388
  8.9 12.8 %all-to-all-start = ((bf16[16,8,128]{2,1,0:T(8,128)(2,1)}), bf16[16,8,128]{2,1,0:T(8,128)(2,1)S(1)}, u32[]{:S(2)}, u32[]{:S(2)}) async-start(bf16[16,8,128]{2,1,0:T(8,128)(2,1)} %shard_map.73), calls=%async_computation | async-start | bytes 65536 | tf_op jit(solution)/shard_map/all_to_all | solution.py:209
  39.1 11.0 %all-to-all-start.2 = ((bf16[16,16,256]{2,1,0:T(8,128)(2,1)}), bf16[16,16,256]{2,1,0:T(8,128)(2,1)S(1)}, u32[]{:S(2)}, u32[]{:S(2)}) async-start(bf16[16,16,256]{2,1,0:T(8,128)(2,1)} %shard_map.77), calls=%async_computation.2 | async-start | bytes 262144 | tf_op jit(solution)/shard_map/all_to_all | solution.py:234
  50.1 42.0 %all-to-all-start.3 = ((bf16[16,256,128]{2,1,0:T(8,128)(2,1)}), bf16[16,256,128]{2,1,0:T(8,128)(2,1)S(1)}, u32[]{:S(2)}, u32[]{:S(2)}) async-start(bf16[16,256,128]{2,1,0:T(8,128)(2,1)} %shard_map.76), calls=%async_computation.3 | async-start | bytes 2097152 | tf_op jit(solution)/shard_map/all_to_all | solution.py:246
  53.8 0.8 copy-start.10
  54.5 3.2 %collective-permute-start.9 = (bf16[2,128,128]{2,1,0:T(8,128)(2,1)S(1)}, bf16[2,128,128]{2,1,0:T(8,128)(2,1)S(1)}, u32[]{:S(2)}, u32[]{:S(2)}) collective-permute-start(bf16[2,128,128]{2,1,0:T(8,128)(2,1)S(1)} %get-tuple-element.20), channel_id=1, source_target_pairs={{0,6},{1,7},{2,0},{3,1},{4,2},{5,3},{6,4},{7,5},{8,14},{9,15},{10,... | collective-permute-start | bytes 196616 | tf_op jit(solution)/shard_map/ppermute | solution.py:182
  55.6 4.3 %collective-permute-start.8 = (bf16[2,128,128]{2,1,0:T(8,128)(2,1)S(1)}, bf16[2,128,128]{2,1,0:T(8,128)(2,1)S(1)}, u32[]{:S(2)}, u32[]{:S(2)}) collective-permute-start(bf16[2,128,128]{2,1,0:T(8,128)(2,1)S(1)} %get-tuple-element.20), channel_id=1, source_target_pairs={{0,2},{1,3},{2,4},{3,5},{4,6},{5,7},{6,0},{7,1},{8,10},{9,11},{10,... | collective-permute-start | bytes 196616 | tf_op jit(solution)/shard_map/ppermute | solution.py:182
  56.1 4.6 %collective-permute-start.10 = (bf16[2,128,128]{2,1,0:T(8,128)(2,1)S(1)}, bf16[2,128,128]{2,1,0:T(8,128)(2,1)S(1)}, u32[]{:S(2)}, u32[]{:S(2)}) collective-permute-start(bf16[2,128,128]{2,1,0:T(8,128)(2,1)S(1)} %get-tuple-element.20), channel_id=1, source_target_pairs={{0,4},{1,5},{2,6},{3,7},{4,0},{5,1},{6,2},{7,3},{8,12},{9,13},{10,... | collective-permute-start | bytes 196616 | tf_op jit(solution)/shard_map/ppermute | solution.py:182
  60.7 17.4 %collective-permute-start.11 = (bf16[4,2,128,128]{3,2,1,0:T(8,128)(2,1)S(1)}, bf16[4,2,128,128]{3,2,1,0:T(8,128)(2,1)S(1)}, u32[]{:S(2)}, u32[]{:S(2)}) collective-permute-start(bf16[4,2,128,128]{3,2,1,0:T(8,128)(2,1)S(1)} %pad_maximum_fusion.refs_8_), channel_id=1, source_target_pairs={{0,8},{1,9},{2,10},{3,11},{4,12},{5,13},{6,14},{7,15},{8,0},{9,1},... | collective-permute-start | bytes 786440 | tf_op jit(solution)/shard_map/ppermute | solution.py:182
  61.9 15.3 %collective-permute-start.1 = (bf16[16,16,256]{2,1,0:T(8,128)(2,1)S(1)}, bf16[16,16,256]{2,1,0:T(8,128)(2,1)S(1)}, u32[]{:S(2)}, u32[]{:S(2)}) collective-permute-start(bf16[16,16,256]{2,1,0:T(8,128)(2,1)S(1)} %shard_map.78.refs_0_), channel_id=1, source_target_pairs={{0,8},{1,9},{2,10},{3,11},{4,12},{5,13},{6,14},{7,15},{8,0},{9,1},... | collective-permute-start | bytes 393224 | tf_op jit(solution)/shard_map/ppermute | solution.py:182
  64.1 16.3 %collective-permute-start.6 = (bf16[16,16,256]{2,1,0:T(8,128)(2,1)S(1)}, bf16[16,16,256]{2,1,0:T(8,128)(2,1)S(1)}, u32[]{:S(2)}, u32[]{:S(2)}) collective-permute-start(bf16[16,16,256]{2,1,0:T(8,128)(2,1)S(1)} %shard_map.78.refs_0_), channel_id=1, source_target_pairs={{0,4},{1,5},{2,6},{3,7},{4,0},{5,1},{6,2},{7,3},{8,12},{9,13},{10,... | collective-permute-start | bytes 393224 | tf_op jit(solution)/shard_map/ppermute | solution.py:182
  65.0 18.8 %collective-permute-start.4 = (bf16[16,16,256]{2,1,0:T(8,128)(2,1)S(1)}, bf16[16,16,256]{2,1,0:T(8,128)(2,1)S(1)}, u32[]{:S(2)}, u32[]{:S(2)}) collective-permute-start(bf16[16,16,256]{2,1,0:T(8,128)(2,1)S(1)} %shard_map.78.refs_0_), channel_id=1, source_target_pairs={{0,6},{1,7},{2,0},{3,1},{4,2},{5,3},{6,4},{7,5},{8,14},{9,15},{10,... | collective-permute-start | bytes 393224 | tf_op jit(solution)/shard_map/ppermute | solution.py:182
  67.1 17.4 %collective-permute-start.2 = (bf16[16,16,256]{2,1,0:T(8,128)(2,1)S(1)}, bf16[16,16,256]{2,1,0:T(8,128)(2,1)S(1)}, u32[]{:S(2)}, u32[]{:S(2)}) collective-permute-start(bf16[16,16,256]{2,1,0:T(8,128)(2,1)S(1)} %shard_map.78.refs_0_), channel_id=1, source_target_pairs={{0,2},{1,3},{2,4},{3,5},{4,6},{5,7},{6,0},{7,1},{8,10},{9,11},{10,... | collective-permute-start | bytes 393224 | tf_op jit(solution)/shard_map/ppermute | solution.py:182
  77.3 7.8 %collective-permute-start.7 = (bf16[16,16,256]{2,1,0:T(8,128)(2,1)S(1)}, bf16[16,16,256]{2,1,0:T(8,128)(2,1)S(1)}, u32[]{:S(2)}, u32[]{:S(2)}) collective-permute-start(bf16[16,16,256]{2,1,0:T(8,128)(2,1)S(1)} %collective-permute-done.1.refs_1_), channel_id=1, source_target_pairs={{0,4},{1,5},{2,6},{3,7},{4,0},{5,1},{6,2},{7,3},{8,12},{9,13},{10,... | collective-permute-start | bytes 393224 | tf_op jit(solution)/shard_map/ppermute | solution.py:182
  78.2 7.6 %collective-permute-start.5 = (bf16[16,16,256]{2,1,0:T(8,128)(2,1)S(1)}, bf16[16,16,256]{2,1,0:T(8,128)(2,1)S(1)}, u32[]{:S(2)}, u32[]{:S(2)}) collective-permute-start(bf16[16,16,256]{2,1,0:T(8,128)(2,1)S(1)} %collective-permute-done.1.refs_1_), channel_id=1, source_target_pairs={{0,6},{1,7},{2,0},{3,1},{4,2},{5,3},{6,4},{7,5},{8,14},{9,15},{10,... | collective-permute-start | bytes 393224 | tf_op jit(solution)/shard_map/ppermute | solution.py:182
  80.4 6.4 %collective-permute-start.3 = (bf16[16,16,256]{2,1,0:T(8,128)(2,1)S(1)}, bf16[16,16,256]{2,1,0:T(8,128)(2,1)S(1)}, u32[]{:S(2)}, u32[]{:S(2)}) collective-permute-start(bf16[16,16,256]{2,1,0:T(8,128)(2,1)S(1)} %collective-permute-done.1.refs_1_), channel_id=1, source_target_pairs={{0,2},{1,3},{2,4},{3,5},{4,6},{5,7},{6,0},{7,1},{8,10},{9,11},{10,... | collective-permute-start | bytes 393224 | tf_op jit(solution)/shard_map/ppermute | solution.py:182
  83.8 0.6 copy-start
  84.5 0.7 copy-start.2
  85.1 0.7 copy-start.4
  85.8 0.6 copy-start.6
  86.8 0.7 copy-start.8
  87.5 0.9 copy-start.1
  88.4 0.9 copy-start.3
  89.3 0.9 copy-start.5
  90.2 0.9 copy-start.7
  91.1 0.9 copy-start.9
  93.4 4.9 %collective-permute-start.12 = (bf16[2,128,128]{2,1,0:T(8,128)(2,1)S(1)}, bf16[2,128,128]{2,1,0:T(8,128)(2,1)S(1)}, u32[]{:S(2)}, u32[]{:S(2)}) collective-permute-start(bf16[2,128,128]{2,1,0:T(8,128)(2,1)S(1)} %shard_map.81), channel_id=1, source_target_pairs={{0,1},{1,0},{2,3},{3,2},{4,5},{5,4},{6,7},{7,6},{8,9},{9,8},{10,11... | collective-permute-start | bytes 196616 | tf_op jit(solution)/shard_map/ppermute | solution.py:283

commit v2 on v1

v2 whole, which is shorter than its diff:
```python
import jax
import jax.numpy as jnp
from jax import lax
from jax.experimental import pallas as pl
from jax.experimental.pallas import tpu as pltpu
from jax.sharding import PartitionSpec as P


BF = jnp.bfloat16
F32 = jnp.float32
I32 = jnp.int32
COLS = 16
LIMIT = 16 << 20
PLACES = ((0, 0), (1, 0), (0, 1), (1, 1), (0, 3), (1, 3), (0, 2), (1, 2))
SMEM = pl.BlockSpec(memory_space=pltpu.SMEM)
VMEM = pl.BlockSpec(memory_space=pltpu.VMEM)
ANY = pl.BlockSpec(memory_space=pl.ANY)


def iota(shape, dim):
    return lax.broadcasted_iota(I32, shape, dim)


def hot(cond):
    return jnp.where(cond, 1.0, 0.0).astype(BF)


def dot(a, b):
    return jnp.dot(a, b, preferred_element_type=F32)


def name_kernel(slab_idx, pattern, send):
    lane = iota((8, 128), 1)
    line = jnp.where(lane == 0, slab_idx[0:1, 0:1], jnp.where(lane == 1, pattern[0:1, 0:1], pattern[0:1, 1:2]))
    send[...] = jnp.broadcast_to(line.astype(F32).astype(BF)[None], send.shape)


def split_kernel(ham, coef, send, turned, part, sem):
    col = lax.axis_index("col")
    chip, core = col // 2, col % 2
    copy = pltpu.make_async_copy(ham.at[:, :, pl.ds(pl.multiple_of(chip * 16, 16), 16), :], part, sem)
    copy.start()
    for j in range(4):
        turned[j] = coef[j, 0].T
    a, b = iota((128, 128), 0), iota((128, 128), 1)
    order = hot((a // 8 == b % 16) & (a % 8 == b // 16))
    first = hot((b < 64) & (a == b + 64 * core))
    second = hot((b >= 64) & (a == b - 64 + 64 * core))
    copy.wait()
    for s in range(2):
        left = part[:, 2 * s].reshape(128, 128)
        right = part[:, 2 * s + 1].reshape(128, 128)
        half = (dot(left, first) + dot(right, second)).astype(BF)
        send[:, :, s * 128 : (s + 1) * 128] = dot(order, half).reshape(16, 8, 128).astype(BF)


def stamp_kernel(ham_idx, coef_idx, named, parts, send):
    send[:, :, 0:256] = parts[...]
    lane, line = iota((8, 128), 1), iota((8, 128), 0)
    meta = jnp.zeros((8, 128), I32)
    for p in range(8):
        for k in range(4):
            meta = jnp.where((line == p) & (lane == k), ham_idx[p, k], meta)
    for j in range(4):
        meta = jnp.where(lane == 4 + j, coef_idx[j, 0], meta)
    a, b = iota((128, 128), 0), iota((128, 128), 1)
    flat = named[...].astype(F32).reshape(128, 128).astype(BF)
    slabs = (b >= 16) & (b < 32)
    pats = (b >= 32) & (b < 64)
    src = jnp.where(slabs, 0, 1 + b % 2)
    at = jnp.where(slabs, b - 16, (b - 32) // 2)
    picked = dot(flat, hot((slabs | pats) & (a == src)))
    line_all = jnp.sum(jnp.where(a == 8 * at, picked, 0.0), axis=0, keepdims=True)
    meta = meta.astype(F32) + line_all
    send[:, :, 256:384] = jnp.broadcast_to(meta.astype(BF)[None], (16, 8, 128))


def pick_kernel(got, send):
    pieces = got[:, :, 0:256].astype(F32).reshape(128, 256).astype(BF)
    flat = got[:, :, 256:384].astype(F32).reshape(128, 128).astype(BF)
    a, b = iota((16, 128), 0), iota((16, 128), 1)
    names = lax.dot_general(hot(b == 16 + a), flat, (((1,), (1,)), ((), ())), preferred_element_type=F32)
    lane = b.astype(F32)
    picks = jnp.concatenate(
        [jnp.where(names[:, 8 * r : 8 * r + 1] == lane, 1.0, 0.0) for r in range(16)], axis=0
    )
    send[...] = dot(picks.astype(BF), pieces).astype(BF).reshape(16, 16, 256)


def pack_kernel(got, piece):
    a, b = iota((256, 256), 0), iota((256, 256), 1)
    order = hot((a // 16 == b % 16) & (a % 16 == b // 16))
    piece[...] = dot(order, got[...].reshape(256, 256)).astype(BF).reshape(16, 16, 256)


def choose_kernel(tables, turned, send):
    col = lax.axis_index("col")
    for r in range(16):
        for e in range(2):
            send[r, 128 * e : 128 * e + 128] = turned[tables[r, 32 + 2 * col + e] - 4 * col]


def match_kernel(ham_names, tables, out, slots):
    row, col = lax.axis_index("row"), lax.axis_index("col")

    def clear(q, _):
        for i in range(32):
            slots[q * 32 + i] = -1
        return 0

    lax.fori_loop(0, 8, clear, 0)
    for e in range(2):
        base = 4 + tables[row, 32 + 2 * col + e] - 4 * col
        for m in range(16):
            slots[e * 128 + tables[m, base]] = m
    for m in range(16):
        p = tables[row, 16 + m]
        for k in range(4):
            q = ham_names[p, k]
            for e in range(2):
                out[m * 8 + k * 2 + e] = jnp.where(q >= 0, slots[e * 128 + jnp.maximum(q, 0)], -1)


def gather_kernel(*refs):
    hams, ham = refs[:8], refs[8]
    chip = lax.axis_index("col") // 2
    x, y = chip // 4, chip % 4
    for t, (dx, dy) in enumerate(PLACES):
        s = ((x + dx) % 2) * 4 + (y - dy + 4) % 4
        ham[:, pl.ds(pl.multiple_of(s * 16, 16), 16), :] = hams[t][...]


def product_kernel(match, coefs, ham, across, near_slabs, far_slabs, out, image, chosen):
    col = lax.axis_index("col")
    chip, core = col // 2, col % 2
    x, y = chip // 4, chip % 4
    for m in range(16):
        for k in range(4):
            for e in range(2):
                slot = match[m * 8 + k * 2 + e]
                for h in range(2):
                    half = core if h == 0 else 1 - core
                    at = pl.ds(pl.multiple_of(128 * e + 64 * half, 64), 64)
                    found = coefs[jnp.maximum(slot, 0), at]
                    chosen[m % 2, h, k * 64 : k * 64 + 64, e * 128 : e * 128 + 128] = jnp.where(
                        slot >= 0, found, jnp.zeros_like(found)
                    )
        image[m // 2, 128 * (m % 2) : 128 * (m % 2) + 128] = (dot(ham[m], chosen[m % 2, 0]) + dot(across[m], chosen[m % 2, 1])).astype(BF)
    total = jnp.zeros((128, 256), F32)
    for s in range(8):
        d = (y - s % 4 + 4) % 4
        two = [jnp.where(x == s // 4, near_slabs[d, (h + core) % 2], far_slabs[d, (h + core) % 2]) for h in range(2)]
        total = total + dot(jnp.concatenate(two, axis=1), image[s])
    for e in range(2):
        out[0, e] = total[:, e * 128 : e * 128 + 128].astype(BF)


def shift(value, dx, dy):
    pairs = [
        (x * 8 + y * 2 + k, ((x + dx) % 2) * 8 + ((y + dy) % 4) * 2 + k)
        for x in range(2)
        for y in range(4)
        for k in range(2)
    ]
    return lax.ppermute(value, "col", pairs)


def near(value):
    return pltpu.with_memory_space_constraint(value, pltpu.VMEM)


def run(kernel, outs, specs, args, scratch=(), limit=None):
    args = [near(v) if spec == "near" else v for spec, v in zip(specs, args)]
    specs = [VMEM if spec == "near" else spec for spec in specs]
    single = not isinstance(outs, list)
    outs = [outs] if single else outs
    result = pl.pallas_call(
        kernel,
        out_shape=[pltpu.VMEM(shape, kind) for shape, kind in outs],
        in_specs=specs,
        out_specs=[VMEM] * len(outs),
        scratch_shapes=scratch,
        compiler_params=pltpu.CompilerParams(vmem_limit_bytes=limit),
    )(*args)
    return result[0] if single else result


def body(ham_blocks, ham_index, coef_blocks, coef_index, slab_blocks, slab_index, pattern_index):
    cores = [(i, i ^ 1) for i in range(COLS)]

    names = run(name_kernel, ((COLS, 8, 128), BF), [VMEM, VMEM], [slab_index, pattern_index])
    named = lax.all_to_all(names, "col", 0, 0)

    parts, turned = run(
        split_kernel,
        [((16, 8, 256), BF), ((4, 128, 128), BF)],
        [ANY, VMEM],
        [ham_blocks, coef_blocks],
        [pltpu.VMEM((8, 4, 16, 128), BF), pltpu.SemaphoreType.DMA],
    )
    swapped = lax.ppermute(slab_blocks[0, 0], "col", cores)

    stamped = run(stamp_kernel, ((16, 8, 384), BF), [SMEM, SMEM, "near", "near"], [ham_index, coef_index, named, parts])
    got = lax.all_to_all(stamped, "row", 0, 0)

    pair = jnp.stack([slab_blocks[0, 0], swapped])
    line = [pair] + [shift(pair, 0, d) for d in (1, 2, 3)]
    line = jnp.stack(line)
    slabs = [line, shift(line, 1, 0)]

    picked = run(pick_kernel, ((16, 16, 256), BF), ["near"], [got])
    picks = lax.all_to_all(picked, "row", 0, 0)

    numbers = got[:, 0, 256:384].astype(I32)
    ham_names = got[:, :, 256:260].reshape(128, 4).astype(I32)
    wanted = run(choose_kernel, ((16, 256, 128), BF), [SMEM, "near"], [numbers, turned], limit=LIMIT)
    wanted, picks = lax.optimization_barrier((wanted, picks))
    coefs = lax.all_to_all(wanted, "row", 0, 0)

    piece = run(pack_kernel, ((16, 16, 256), BF), ["near"], [picks], limit=LIMIT)
    across = shift(piece, 1, 0)
    hams = [piece, across]
    for d in (1, 3, 2):
        hams += [shift(piece, 0, d), shift(across, 0, d)]

    match = pl.pallas_call(
        match_kernel,
        out_shape=pltpu.SMEM((128,), I32),
        in_specs=[SMEM] * 2,
        out_specs=SMEM,
        scratch_shapes=[pltpu.SMEM((256,), I32)],
        compiler_params=pltpu.CompilerParams(vmem_limit_bytes=LIMIT),
        name="match",
    )(ham_names, numbers)
    match = pltpu.with_memory_space_constraint(match, pltpu.SMEM)

    ham = run(gather_kernel, ((16, 128, 256), BF), ["near"] * 8, hams, limit=LIMIT)
    across = lax.ppermute(ham, "col", cores)
    return pl.pallas_call(
        product_kernel,
        out_shape=jax.ShapeDtypeStruct((1, 2, 128, 128), BF),
        in_specs=[SMEM] + [VMEM] * 5,
        out_specs=VMEM,
        scratch_shapes=[pltpu.VMEM((8, 256, 256), BF), pltpu.VMEM((2, 2, 256, 256), BF)],
        compiler_params=pltpu.CompilerParams(vmem_limit_bytes=LIMIT),
        name="product",
    )(match, near(coefs), near(ham), near(across), near(slabs[0]), near(slabs[1]))


def solution(mesh):
    placed = (
        P("row", None, None, None),
        P("row", None),
        P("col", "row", None, None),
        P("col", "row"),
        P("row", "col", None, None),
        P("row", "col"),
        P("row", "col"),
    )
    return jax.shard_map(body, mesh=mesh, in_specs=placed, out_specs=P("row", "col", None, None), check_vma=False)
```

time: 99.7 us -> 93.7 us (0.940)
  local copies, waits for them, and re-layouts: 10.5 us -> 3 us
  waiting for transfers between devices: 26 us -> 32.5 us
  starting transfers between devices: 31.2 us -> 28.4 us
  other arithmetic: 1.93 us -> 0.06 us
    unnamed x26 -> x12, local copies, waits for them, and re-layouts: 10.5 us -> 3 us
    ppermute x11, waiting for transfers between devices: 14.3 us -> 20.9 us  [shift(): return lax.ppermute(value, 'col', pairs)]
    ppermute x2, starting transfers between devices: 6.9 us -> 1.94 us  [the longest x1 1.83 us: body(): across = lax.ppermute(ham, 'col', cores)]
    all_to_all x1, starting transfers between devices: 5.48 us -> 8.57 us  [body(): named = lax.all_to_all(names, 'col', 0, 0)]
    all_to_all x1, waiting for transfers between devices: 6.63 us -> 3.64 us  [body(): named = lax.all_to_all(names, 'col', 0, 0)]
    pallas_call x9 -> x7, Pallas kernels: 10.2 us -> 7.63 us  [run(): pl.pallas_call(kernel, out_shape=[pltpu.VMEM(shape, kind) for shape, kind...]
    ppermute x2, waiting for transfers between devices: 0.01 us -> 2.23 us  [the longest x1 2.22 us: body(): swapped = lax.ppermute(slab_blocks[0, 0], 'col', cores)]
    pallas_call x1 -> x2, Pallas kernels: 2.75 us -> 4.85 us  [the longest x1 2.59 us: body(): pl.pallas_call(product_kernel, out_shape=jax.ShapeDtypeStruct((1, 2, 128,...]
  transfers between devices with their start and end apart: 16 -> 16, of which waited for: 7 -> 10; matrix products, arithmetic and copies ran while one was open for 2% -> 2% of each run, Pallas kernels for 8% -> 7%
where the time goes in v2:
time: 93.7 us; the launch traced here: 92.7 us
  waiting for transfers between devices  32.5 us (35%)
  starting transfers between devices  28.4 us (30%)
  blocking collectives  15.5 us (17%)
  Pallas kernels  12.5 us (13%)
  local copies, waits for them, and re-layouts  3 us (3%)
    ppermute x11, waiting for transfers between devices, shift(): return lax.ppermute(value, 'col', pairs)  20.9 us
    all_to_all x1, blocking collectives, body(): got = lax.all_to_all(stamped, 'row', 0, 0)  15.5 us
    ppermute x11, starting transfers between devices, shift(): return lax.ppermute(value, 'col', pairs)  10.7 us
    all_to_all x1, starting transfers between devices, body(): named = lax.all_to_all(names, 'col', 0, 0)  8.57 us
    pallas_call x7, Pallas kernels, run(): pl.pallas_call(kernel, out_shape=[pltpu.VMEM(shape, kind) for shape, kind...  7.63 us
    all_to_all x1, waiting for transfers between devices, body(): picks = lax.all_to_all(picked, 'row', 0, 0)  5.7 us
    all_to_all x1, starting transfers between devices, body(): coefs = lax.all_to_all(wanted, 'row', 0, 0)  3.65 us
    all_to_all x1, waiting for transfers between devices, body(): named = lax.all_to_all(names, 'col', 0, 0)  3.64 us
  transfers between devices with their start and end apart: 16, of which 10 were waited for; matrix products, arithmetic and copies ran while one was open for 2% of the time, Pallas kernels for 7%

profile of v2, /device:TPU:1, one launch (start us, length us, event | category | flops | bytes accessed | tf_op | source)
XLA Modules:
  0.0 92.7 jit_solution(13227361007822574325)
XLA Ops:
  0.7 1.3 %shard_map.73 = bf16[16,8,128]{2,1,0:T(8,128)(2,1)} custom-call(s32[1,1]{1,0:T(1,128)S(6)} %copy.10.slab_idx, s32[1,2]{1,0:T(1,128)} %pattern.1), custom_call_target="tpu_custom_call" | custom-call | tf_op jit(solution)/shard_map/pallas_call | solution.py:177
  2.0 8.6 %all-to-all-start = ((bf16[16,8,128]{2,1,0:T(8,128)(2,1)}), bf16[16,8,128]{2,1,0:T(8,128)(2,1)S(1)}, u32[]{:S(2)}, u32[]{:S(2)}) async-start(bf16[16,8,128]{2,1,0:T(8,128)(2,1)} %shard_map.73), calls=%async_computation | async-start | bytes 65536 | tf_op jit(solution)/shard_map/all_to_all | solution.py:192
  10.6 0.7 copy.9.coef_idx
  11.3 0.7 copy.8.ham_idx
  11.9 2.3 %shard_map.74 = (bf16[16,8,256]{2,1,0:T(8,128)(2,1)S(1)}, bf16[4,128,128]{2,1,0:T(8,128)(2,1)S(1)}) custom-call(bf16[8,4,128,128]{3,2,1,0:T(8,128)(2,1)} %ham.1, bf16[4,1,128,128]{3,2,1,0:T(8,128)(2,1)} %coef.1), custom_call_target="tpu_custom_call" | custom-call | tf_op jit(solution)/shard_map/pallas_call | solution.py:177
  14.2 3.6 %all-to-all-done.named = bf16[16,8,128]{2,1,0:T(8,128)(2,1)S(1)} async-done(((bf16[16,8,128]{2,1,0:T(8,128)(2,1)}), bf16[16,8,128]{2,1,0:T(8,128)(2,1)S(1)}, u32[]{:S(2)}, u32[]{:S(2)}) %all-to-all-start) | async-done | bytes 32800 | tf_op jit(solution)/shard_map/all_to_all | solution.py:192
  17.9 0.9 shard_map.75
  18.8 15.5 %all_to_all.20.got = bf16[16,8,384]{2,1,0:T(8,128)(2,1)S(1)} all-to-all(bf16[16,8,384]{2,1,0:T(8,128)(2,1)S(1)} %shard_map.75), channel_id=1, replica_groups=mesh['row'=16,'col'=16] {'row'}, dimensions={0} | all-to-all | bytes 196608 | tf_op jit(solution)/shard_map/all_to_all | solution.py:204
  34.3 1.0 %shard_map.77 = bf16[16,16,256]{2,1,0:T(8,128)(2,1)} custom-call(bf16[16,8,384]{2,1,0:T(8,128)(2,1)S(1)} %all_to_all.20.got), custom_call_target="tpu_custom_call" | custom-call | tf_op jit(solution)/shard_map/pallas_call | solution.py:177
  35.3 3.5 %all-to-all-start.2 = ((bf16[16,16,256]{2,1,0:T(8,128)(2,1)}), bf16[16,16,256]{2,1,0:T(8,128)(2,1)S(1)}, u32[]{:S(2)}, u32[]{:S(2)}) async-start(bf16[16,16,256]{2,1,0:T(8,128)(2,1)} %shard_map.77), calls=%async_computation.2 | async-start | bytes 262144 | tf_op jit(solution)/shard_map/all_to_all | solution.py:212
  38.9 1.8 %shard_map.76 = bf16[16,256,128]{2,1,0:T(8,128)(2,1)} custom-call(s32[16,128]{1,0:T(8,128)S(1)} %bitcast.14, bf16[4,128,128]{2,1,0:T(8,128)(2,1)S(1)} %get-tuple-element.10.turned), custom_call_target="tpu_custom_call" | custom-call | tf_op jit(solution)/shard_map/pallas_call | solution.py:177
  40.6 5.7 %all-to-all-done.2.got = bf16[16,16,256]{2,1,0:T(8,128)(2,1)S(1)} async-done(((bf16[16,16,256]{2,1,0:T(8,128)(2,1)}), bf16[16,16,256]{2,1,0:T(8,128)(2,1)S(1)}, u32[]{:S(2)}, u32[]{:S(2)}) %all-to-all-start.2) | async-done | bytes 131104 | tf_op jit(solution)/shard_map/all_to_all | solution.py:212
  46.3 3.7 %all-to-all-start.3 = ((bf16[16,256,128]{2,1,0:T(8,128)(2,1)}), bf16[16,256,128]{2,1,0:T(8,128)(2,1)S(1)}, u32[]{:S(2)}, u32[]{:S(2)}) async-start(bf16[16,256,128]{2,1,0:T(8,128)(2,1)} %shard_map.76), calls=%async_computation.3 | async-start | bytes 2097152 | tf_op jit(solution)/shard_map/all_to_all | solution.py:218
  50.2 1.0 %collective-permute-start = (bf16[16,16,256]{2,1,0:T(8,128)(2,1)S(1)}, bf16[16,16,256]{2,1,0:T(8,128)(2,1)S(1)}, u32[]{:S(2)}, u32[]{:S(2)}) collective-permute-start(bf16[16,16,256]{2,1,0:T(8,128)(2,1)S(1)} %shard_map.78.refs_0_), channel_id=1, source_target_pairs={{0,8},{1,9},{2,10},{3,11},{4,12},{5,13},{6,14},{7,15},{8,0},{9,1},... | collective-permute-start | bytes 393224 | tf_op jit(solution)/shard_map/ppermute | solution.py:165
  51.2 1.6 %collective-permute-start.5 = (bf16[16,16,256]{2,1,0:T(8,128)(2,1)S(1)}, bf16[16,16,256]{2,1,0:T(8,128)(2,1)S(1)}, u32[]{:S(2)}, u32[]{:S(2)}) collective-permute-start(bf16[16,16,256]{2,1,0:T(8,128)(2,1)S(1)} %shard_map.78.refs_0_), channel_id=1, source_target_pairs={{0,4},{1,5},{2,6},{3,7},{4,0},{5,1},{6,2},{7,3},{8,12},{9,13},{10,... | collective-permute-start | bytes 393224 | tf_op jit(solution)/shard_map/ppermute | solution.py:165
  52.8 1.1 %collective-permute-start.3 = (bf16[16,16,256]{2,1,0:T(8,128)(2,1)S(1)}, bf16[16,16,256]{2,1,0:T(8,128)(2,1)S(1)}, u32[]{:S(2)}, u32[]{:S(2)}) collective-permute-start(bf16[16,16,256]{2,1,0:T(8,128)(2,1)S(1)} %shard_map.78.refs_0_), channel_id=1, source_target_pairs={{0,6},{1,7},{2,0},{3,1},{4,2},{5,3},{6,4},{7,5},{8,14},{9,15},{10,... | collective-permute-start | bytes 393224 | tf_op jit(solution)/shard_map/ppermute | solution.py:165
  54.3 5.2 %collective-permute-done.refs_1_ = bf16[16,16,256]{2,1,0:T(8,128)(2,1)S(1)} collective-permute-done((bf16[16,16,256]{2,1,0:T(8,128)(2,1)S(1)}, bf16[16,16,256]{2,1,0:T(8,128)(2,1)S(1)}, u32[]{:S(2)}, u32[]{:S(2)}) %collective-permute-start) | collective-permute-done | bytes 131104 | tf_op jit(solution)/shard_map/ppermute | solution.py:165
  59.5 2.7 %collective-permute-start.4 = (bf16[16,16,256]{2,1,0:T(8,128)(2,1)S(1)}, bf16[16,16,256]{2,1,0:T(8,128)(2,1)S(1)}, u32[]{:S(2)}, u32[]{:S(2)}) collective-permute-start(bf16[16,16,256]{2,1,0:T(8,128)(2,1)S(1)} %collective-permute-done.refs_1_), channel_id=1, source_target_pairs={{0,6},{1,7},{2,0},{3,1},{4,2},{5,3},{6,4},{7,5},{8,14},{9,15},{10,... | collective-permute-start | bytes 393224 | tf_op jit(solution)/shard_map/ppermute | solution.py:165
  62.2 2.9 %collective-permute-done.6.refs_7_ = bf16[16,16,256]{2,1,0:T(8,128)(2,1)S(1)} collective-permute-done((bf16[16,16,256]{2,1,0:T(8,128)(2,1)S(1)}, bf16[16,16,256]{2,1,0:T(8,128)(2,1)S(1)}, u32[]{:S(2)}, u32[]{:S(2)}) %collective-permute-start.6) | collective-permute-done | bytes 131104 | tf_op jit(solution)/shard_map/ppermute | solution.py:165
  65.7 3.0 %collective-permute-done.2.refs_3_ = bf16[16,16,256]{2,1,0:T(8,128)(2,1)S(1)} collective-permute-done((bf16[16,16,256]{2,1,0:T(8,128)(2,1)S(1)}, bf16[16,16,256]{2,1,0:T(8,128)(2,1)S(1)}, u32[]{:S(2)}, u32[]{:S(2)}) %collective-permute-start.2) | collective-permute-done | bytes 131104 | tf_op jit(solution)/shard_map/ppermute | solution.py:165
  68.9 1.8 %collective-permute-start.7 = (bf16[16,128,256]{2,1,0:T(8,128)(2,1)S(1)}, bf16[16,128,256]{2,1,0:T(8,128)(2,1)S(1)}, u32[]{:S(2)}, u32[]{:S(2)}) collective-permute-start(bf16[16,128,256]{2,1,0:T(8,128)(2,1)S(1)} %shard_map.79.ham), channel_id=1, source_target_pairs={{0,1},{1,0},{2,3},{3,2},{4,5},{5,4},{6,7},{7,6},{8,9},{9,8},{10,11... | collective-permute-start | bytes 3145736 | tf_op jit(solution)/shard_map/ppermute | solution.py:238
  70.8 2.2 %collective-permute-done.8 = bf16[128,128]{1,0:T(8,128)(2,1)S(1)} collective-permute-done((bf16[128,128]{1,0:T(8,128)(2,1)S(1)}, bf16[128,128]{1,0:T(8,128)(2,1)S(1)}, u32[]{:S(2)}, u32[]{:S(2)}) %collective-permute-start.8) | collective-permute-done | bytes 32800 | tf_op jit(solution)/shard_map/ppermute | solution.py:201
  73.3 0.6 collective-permute-start.9
  73.9 2.1 %collective-permute-start.11 = (bf16[2,128,128]{2,1,0:T(8,128)(2,1)S(1)}, bf16[2,128,128]{2,1,0:T(8,128)(2,1)S(1)}, u32[]{:S(2)}, u32[]{:S(2)}) collective-permute-start(bf16[2,128,128]{2,1,0:T(8,128)(2,1)S(1)} %get-tuple-element.14), channel_id=1, source_target_pairs={{0,6},{1,7},{2,0},{3,1},{4,2},{5,3},{6,4},{7,5},{8,14},{9,15},{10,... | collective-permute-start | bytes 196616 | tf_op jit(solution)/shard_map/ppermute | solution.py:165
  76.0 1.9 %collective-permute-done.10 = bf16[2,128,128]{2,1,0:T(8,128)(2,1)S(1)} collective-permute-done((bf16[2,128,128]{2,1,0:T(8,128)(2,1)S(1)}, bf16[2,128,128]{2,1,0:T(8,128)(2,1)S(1)}, u32[]{:S(2)}, u32[]{:S(2)}) %collective-permute-start.10) | collective-permute-done | bytes 65568 | tf_op jit(solution)/shard_map/ppermute | solution.py:165
  77.8 1.8 %collective-permute-done.9 = bf16[2,128,128]{2,1,0:T(8,128)(2,1)S(1)} collective-permute-done((bf16[2,128,128]{2,1,0:T(8,128)(2,1)S(1)}, bf16[2,128,128]{2,1,0:T(8,128)(2,1)S(1)}, u32[]{:S(2)}, u32[]{:S(2)}) %collective-permute-start.9) | collective-permute-done | bytes 65568 | tf_op jit(solution)/shard_map/ppermute | solution.py:165
  79.7 1.0 %collective-permute-start.12 = (bf16[4,2,128,128]{3,2,1,0:T(8,128)(2,1)S(1)}, bf16[4,2,128,128]{3,2,1,0:T(8,128)(2,1)S(1)}, u32[]{:S(2)}, u32[]{:S(2)}) collective-permute-start(bf16[4,2,128,128]{3,2,1,0:T(8,128)(2,1)S(1)} %pad_maximum_fusion.near_slabs), channel_id=1, source_target_pairs={{0,8},{1,9},{2,10},{3,11},{4,12},{5,13},{6,14},{7,15},{8,0},{9,1},... | collective-permute-start | bytes 786440 | tf_op jit(solution)/shard_map/ppermute | solution.py:165
  80.8 2.3 %match.1 = s32[128]{0:T(128)S(4)} custom-call(s32[128,4]{1,0:T(8,128)S(1)} %fusion.ham_names, s32[16,128]{1,0:T(8,128)S(1)} %bitcast.15), custom_call_target="tpu_custom_call" | custom-call | tf_op jit(solution)/shard_map/match/pallas_call | solution.py:226
  83.0 5.4 %collective-permute-done.12.far_slabs = bf16[4,2,128,128]{3,2,1,0:T(8,128)(2,1)S(1)} collective-permute-done((bf16[4,2,128,128]{3,2,1,0:T(8,128)(2,1)S(1)}, bf16[4,2,128,128]{3,2,1,0:T(8,128)(2,1)S(1)}, u32[]{:S(2)}, u32[]{:S(2)}) %collective-permute-start.12) | collective-permute-done | bytes 262176 | tf_op jit(solution)/shard_map/ppermute | solution.py:165
  88.5 0.7 copy-done
  89.2 0.9 %copy-done.1 = bf16[4,2,128,128]{3,2,1,0:T(8,128)(2,1)S(1)} copy-done((bf16[4,2,128,128]{3,2,1,0:T(8,128)(2,1)S(1)}, bf16[4,2,128,128]{3,2,1,0:T(8,128)(2,1)}, u32[]{:S(2)}) %copy-start.1) | copy-done | bytes 262168
  90.1 2.6 %product.1 = bf16[1,2,128,128]{3,2,1,0:T(8,128)(2,1)} custom-call(s32[128]{0:T(128)S(4)} %match.1, bf16[16,256,128]{2,1,0:T(8,128)(2,1)S(1)} %all-to-all-done.3.coefs, bf16[16,128,256]{2,1,0:T(8,128)(2,1)S(1)} %shard_map.79.ham, bf16[16,128,256]{2,1,0:T(8,128)(2,1)S(1)} %collective-permute-done.7.across, ...), custom_call_target="tpu_custom_call" | custom-call | tf_op jit(solution)/shard_map/product/pallas_call | solution.py:239
  (26 shorter events, 1.8 us)
Async XLA Ops:
  2.0 8.6 %copy-start.4 = (s32[4,1]{0,1:T(1,128)S(1)}, s32[4,1]{0,1:T(1,128)}, u32[]{:S(2)}) copy-start(s32[4,1]{0,1:T(1,128)} %param.10) | copy-start | bytes 52
  2.0 15.9 %all-to-all-start = ((bf16[16,8,128]{2,1,0:T(8,128)(2,1)}), bf16[16,8,128]{2,1,0:T(8,128)(2,1)S(1)}, u32[]{:S(2)}, u32[]{:S(2)}) async-start(bf16[16,8,128]{2,1,0:T(8,128)(2,1)} %shard_map.73), calls=%async_computation | async-start | bytes 65536 | tf_op jit(solution)/shard_map/all_to_all | solution.py:192
  10.6 0.7 copy-start.3
  35.3 11.0 %all-to-all-start.2 = ((bf16[16,16,256]{2,1,0:T(8,128)(2,1)}), bf16[16,16,256]{2,1,0:T(8,128)(2,1)S(1)}, u32[]{:S(2)}, u32[]{:S(2)}) async-start(bf16[16,16,256]{2,1,0:T(8,128)(2,1)} %shard_map.77), calls=%async_computation.2 | async-start | bytes 262144 | tf_op jit(solution)/shard_map/all_to_all | solution.py:212
  46.3 42.8 %all-to-all-start.3 = ((bf16[16,256,128]{2,1,0:T(8,128)(2,1)}), bf16[16,256,128]{2,1,0:T(8,128)(2,1)S(1)}, u32[]{:S(2)}, u32[]{:S(2)}) async-start(bf16[16,256,128]{2,1,0:T(8,128)(2,1)} %shard_map.76), calls=%async_computation.3 | async-start | bytes 2097152 | tf_op jit(solution)/shard_map/all_to_all | solution.py:218
  50.2 20.5 %copy-start.2 = (bf16[1,1,128,128]{3,2,1,0:T(8,128)(2,1)S(1)}, bf16[1,1,128,128]{3,2,1,0:T(8,128)(2,1)}, u32[]{:S(2)}) copy-start(bf16[1,1,128,128]{3,2,1,0:T(8,128)(2,1)} %param.11) | copy-start | bytes 98308
  50.2 9.3 %collective-permute-start = (bf16[16,16,256]{2,1,0:T(8,128)(2,1)S(1)}, bf16[16,16,256]{2,1,0:T(8,128)(2,1)S(1)}, u32[]{:S(2)}, u32[]{:S(2)}) collective-permute-start(bf16[16,16,256]{2,1,0:T(8,128)(2,1)S(1)} %shard_map.78.refs_0_), channel_id=1, source_target_pairs={{0,8},{1,9},{2,10},{3,11},{4,12},{5,13},{6,14},{7,15},{8,0},{9,1},... | collective-permute-start | bytes 393224 | tf_op jit(solution)/shard_map/ppermute | solution.py:165
  51.2 11.0 %collective-permute-start.5 = (bf16[16,16,256]{2,1,0:T(8,128)(2,1)S(1)}, bf16[16,16,256]{2,1,0:T(8,128)(2,1)S(1)}, u32[]{:S(2)}, u32[]{:S(2)}) collective-permute-start(bf16[16,16,256]{2,1,0:T(8,128)(2,1)S(1)} %shard_map.78.refs_0_), channel_id=1, source_target_pairs={{0,4},{1,5},{2,6},{3,7},{4,0},{5,1},{6,2},{7,3},{8,12},{9,13},{10,... | collective-permute-start | bytes 393224 | tf_op jit(solution)/shard_map/ppermute | solution.py:165
  52.8 9.4 %collective-permute-start.3 = (bf16[16,16,256]{2,1,0:T(8,128)(2,1)S(1)}, bf16[16,16,256]{2,1,0:T(8,128)(2,1)S(1)}, u32[]{:S(2)}, u32[]{:S(2)}) collective-permute-start(bf16[16,16,256]{2,1,0:T(8,128)(2,1)S(1)} %shard_map.78.refs_0_), channel_id=1, source_target_pairs={{0,6},{1,7},{2,0},{3,1},{4,2},{5,3},{6,4},{7,5},{8,14},{9,15},{10,... | collective-permute-start | bytes 393224 | tf_op jit(solution)/shard_map/ppermute | solution.py:165
  53.9 8.3 %collective-permute-start.1 = (bf16[16,16,256]{2,1,0:T(8,128)(2,1)S(1)}, bf16[16,16,256]{2,1,0:T(8,128)(2,1)S(1)}, u32[]{:S(2)}, u32[]{:S(2)}) collective-permute-start(bf16[16,16,256]{2,1,0:T(8,128)(2,1)S(1)} %shard_map.78.refs_0_), channel_id=1, source_target_pairs={{0,2},{1,3},{2,4},{3,5},{4,6},{5,7},{6,0},{7,1},{8,10},{9,11},{10,... | collective-permute-start | bytes 393224 | tf_op jit(solution)/shard_map/ppermute | solution.py:165
  59.5 5.6 %collective-permute-start.6 = (bf16[16,16,256]{2,1,0:T(8,128)(2,1)S(1)}, bf16[16,16,256]{2,1,0:T(8,128)(2,1)S(1)}, u32[]{:S(2)}, u32[]{:S(2)}) collective-permute-start(bf16[16,16,256]{2,1,0:T(8,128)(2,1)S(1)} %collective-permute-done.refs_1_), channel_id=1, source_target_pairs={{0,4},{1,5},{2,6},{3,7},{4,0},{5,1},{6,2},{7,3},{8,12},{9,13},{10,... | collective-permute-start | bytes 393224 | tf_op jit(solution)/shard_map/ppermute | solution.py:165
  59.5 6.2 %collective-permute-start.4 = (bf16[16,16,256]{2,1,0:T(8,128)(2,1)S(1)}, bf16[16,16,256]{2,1,0:T(8,128)(2,1)S(1)}, u32[]{:S(2)}, u32[]{:S(2)}) collective-permute-start(bf16[16,16,256]{2,1,0:T(8,128)(2,1)S(1)} %collective-permute-done.refs_1_), channel_id=1, source_target_pairs={{0,6},{1,7},{2,0},{3,1},{4,2},{5,3},{6,4},{7,5},{8,14},{9,15},{10,... | collective-permute-start | bytes 393224 | tf_op jit(solution)/shard_map/ppermute | solution.py:165
  62.2 6.6 %collective-permute-start.2 = (bf16[16,16,256]{2,1,0:T(8,128)(2,1)S(1)}, bf16[16,16,256]{2,1,0:T(8,128)(2,1)S(1)}, u32[]{:S(2)}, u32[]{:S(2)}) collective-permute-start(bf16[16,16,256]{2,1,0:T(8,128)(2,1)S(1)} %collective-permute-done.refs_1_), channel_id=1, source_target_pairs={{0,2},{1,3},{2,4},{3,5},{4,6},{5,7},{6,0},{7,1},{8,10},{9,11},{10,... | collective-permute-start | bytes 393224 | tf_op jit(solution)/shard_map/ppermute | solution.py:165
  68.9 20.3 %collective-permute-start.7 = (bf16[16,128,256]{2,1,0:T(8,128)(2,1)S(1)}, bf16[16,128,256]{2,1,0:T(8,128)(2,1)S(1)}, u32[]{:S(2)}, u32[]{:S(2)}) collective-permute-start(bf16[16,128,256]{2,1,0:T(8,128)(2,1)S(1)} %shard_map.79.ham), channel_id=1, source_target_pairs={{0,1},{1,0},{2,3},{3,2},{4,5},{5,4},{6,7},{7,6},{8,9},{9,8},{10,11... | collective-permute-start | bytes 3145736 | tf_op jit(solution)/shard_map/ppermute | solution.py:238
  70.7 2.3 %collective-permute-start.8 = (bf16[128,128]{1,0:T(8,128)(2,1)S(1)}, bf16[128,128]{1,0:T(8,128)(2,1)S(1)}, u32[]{:S(2)}, u32[]{:S(2)}) collective-permute-start(bf16[128,128]{1,0:T(8,128)(2,1)S(1)} %bitcast.19), channel_id=1, source_target_pairs={{0,1},{1,0},{2,3},{3,2},{4,5},{5,4},{6,7},{7,6},{8,9},{9,8},{10,11... | collective-permute-start | bytes 98312 | tf_op jit(solution)/shard_map/ppermute | solution.py:201
  73.0 4.8 %collective-permute-start.10 = (bf16[2,128,128]{2,1,0:T(8,128)(2,1)S(1)}, bf16[2,128,128]{2,1,0:T(8,128)(2,1)S(1)}, u32[]{:S(2)}, u32[]{:S(2)}) collective-permute-start(bf16[2,128,128]{2,1,0:T(8,128)(2,1)S(1)} %get-tuple-element.14), channel_id=1, source_target_pairs={{0,4},{1,5},{2,6},{3,7},{4,0},{5,1},{6,2},{7,3},{8,12},{9,13},{10,... | collective-permute-start | bytes 196616 | tf_op jit(solution)/shard_map/ppermute | solution.py:165
  73.3 6.4 %collective-permute-start.9 = (bf16[2,128,128]{2,1,0:T(8,128)(2,1)S(1)}, bf16[2,128,128]{2,1,0:T(8,128)(2,1)S(1)}, u32[]{:S(2)}, u32[]{:S(2)}) collective-permute-start(bf16[2,128,128]{2,1,0:T(8,128)(2,1)S(1)} %get-tuple-element.14), channel_id=1, source_target_pairs={{0,2},{1,3},{2,4},{3,5},{4,6},{5,7},{6,0},{7,1},{8,10},{9,11},{10,... | collective-permute-start | bytes 196616 | tf_op jit(solution)/shard_map/ppermute | solution.py:165
  73.9 5.8 %collective-permute-start.11 = (bf16[2,128,128]{2,1,0:T(8,128)(2,1)S(1)}, bf16[2,128,128]{2,1,0:T(8,128)(2,1)S(1)}, u32[]{:S(2)}, u32[]{:S(2)}) collective-permute-start(bf16[2,128,128]{2,1,0:T(8,128)(2,1)S(1)} %get-tuple-element.14), channel_id=1, source_target_pairs={{0,6},{1,7},{2,0},{3,1},{4,2},{5,3},{6,4},{7,5},{8,14},{9,15},{10,... | collective-permute-start | bytes 196616 | tf_op jit(solution)/shard_map/ppermute | solution.py:165
  79.7 8.7 %collective-permute-start.12 = (bf16[4,2,128,128]{3,2,1,0:T(8,128)(2,1)S(1)}, bf16[4,2,128,128]{3,2,1,0:T(8,128)(2,1)S(1)}, u32[]{:S(2)}, u32[]{:S(2)}) collective-permute-start(bf16[4,2,128,128]{3,2,1,0:T(8,128)(2,1)S(1)} %pad_maximum_fusion.near_slabs), channel_id=1, source_target_pairs={{0,8},{1,9},{2,10},{3,11},{4,12},{5,13},{6,14},{7,15},{8,0},{9,1},... | collective-permute-start | bytes 786440 | tf_op jit(solution)/shard_map/ppermute | solution.py:165
  88.5 0.7 copy-start
  89.2 1.0 %copy-start.1 = (bf16[4,2,128,128]{3,2,1,0:T(8,128)(2,1)S(1)}, bf16[4,2,128,128]{3,2,1,0:T(8,128)(2,1)}, u32[]{:S(2)}) copy-start(bf16[4,2,128,128]{3,2,1,0:T(8,128)(2,1)} %copy-done) | copy-start | bytes 786436

commit v3 on v2

--- a/solution.py
+++ b/solution.py
@@ -31,7 +31,7 @@
 
 def name_kernel(slab_idx, pattern, send):
     lane = iota((8, 128), 1)
-    line = jnp.where(lane == 0, slab_idx[0:1, 0:1], jnp.where(lane == 1, pattern[0:1, 0:1], pattern[0:1, 1:2]))
+    line = jnp.where(lane == 0, slab_idx[0], jnp.where(lane == 1, pattern[0, 0], pattern[0, 1]))
     send[...] = jnp.broadcast_to(line.astype(F32).astype(BF)[None], send.shape)
 
 
@@ -60,9 +60,9 @@
     meta = jnp.zeros((8, 128), I32)
     for p in range(8):
         for k in range(4):
-            meta = jnp.where((line == p) & (lane == k), ham_idx[p, k], meta)
+            meta = jnp.where((line == p) & (lane == k), ham_idx[k, p], meta)
     for j in range(4):
-        meta = jnp.where(lane == 4 + j, coef_idx[j, 0], meta)
+        meta = jnp.where(lane == 4 + j, coef_idx[0, j], meta)
     a, b = iota((128, 128), 0), iota((128, 128), 1)
     flat = named[...].astype(F32).reshape(128, 128).astype(BF)
     slabs = (b >= 16) & (b < 32)
@@ -130,10 +130,23 @@
         ham[:, pl.ds(pl.multiple_of(s * 16, 16), 16), :] = hams[t][...]
 
 
-def product_kernel(match, coefs, ham, across, near_slabs, far_slabs, out, image, chosen):
+def slab_kernel(near_slabs, far_slabs, slab):
     col = lax.axis_index("col")
     chip, core = col // 2, col % 2
     x, y = chip // 4, chip % 4
+    for s in range(8):
+        d = (y - s % 4 + 4) % 4
+        for h in range(2):
+            at = (h + core) % 2
+            slab[s, :, 128 * h : 128 * h + 128] = jnp.where(x == s // 4, near_slabs[d, at], far_slabs[d, at])
+
+
+def hold_kernel(across, held):
+    held[...] = across[...]
+
+
+def product_kernel(match, coefs, ham, across, slab, out, image, chosen):
+    core = lax.axis_index("col") % 2
     for m in range(16):
         for k in range(4):
             for e in range(2):
@@ -148,9 +161,7 @@
         image[m // 2, 128 * (m % 2) : 128 * (m % 2) + 128] = (dot(ham[m], chosen[m % 2, 0]) + dot(across[m], chosen[m % 2, 1])).astype(BF)
     total = jnp.zeros((128, 256), F32)
     for s in range(8):
-        d = (y - s % 4 + 4) % 4
-        two = [jnp.where(x == s // 4, near_slabs[d, (h + core) % 2], far_slabs[d, (h + core) % 2]) for h in range(2)]
-        total = total + dot(jnp.concatenate(two, axis=1), image[s])
+        total = total + dot(slab[s], image[s])
     for e in range(2):
         out[0, e] = total[:, e * 128 : e * 128 + 128].astype(BF)
 
@@ -188,7 +199,7 @@
 def body(ham_blocks, ham_index, coef_blocks, coef_index, slab_blocks, slab_index, pattern_index):
     cores = [(i, i ^ 1) for i in range(COLS)]
 
-    names = run(name_kernel, ((COLS, 8, 128), BF), [VMEM, VMEM], [slab_index, pattern_index])
+    names = run(name_kernel, ((COLS, 8, 128), BF), [SMEM, SMEM], [slab_index.reshape(1), pattern_index])
     named = lax.all_to_all(names, "col", 0, 0)
 
     parts, turned = run(
@@ -200,7 +211,12 @@
     )
     swapped = lax.ppermute(slab_blocks[0, 0], "col", cores)
 
-    stamped = run(stamp_kernel, ((16, 8, 384), BF), [SMEM, SMEM, "near", "near"], [ham_index, coef_index, named, parts])
+    stamped = run(
+        stamp_kernel,
+        ((16, 8, 384), BF),
+        [SMEM, SMEM, "near", "near"],
+        [ham_index.T, coef_index.T, named, parts],
+    )
     got = lax.all_to_all(stamped, "row", 0, 0)
 
     pair = jnp.stack([slab_blocks[0, 0], swapped])
@@ -213,7 +229,9 @@
 
     numbers = got[:, 0, 256:384].astype(I32)
     ham_names = got[:, :, 256:260].reshape(128, 4).astype(I32)
-    wanted = run(choose_kernel, ((16, 256, 128), BF), [SMEM, "near"], [numbers, turned], limit=LIMIT)
+    wanted = run(
+        choose_kernel, ((16, 256, 128), BF), [SMEM, "near"], [numbers, turned], limit=LIMIT
+    )
     wanted, picks = lax.optimization_barrier((wanted, picks))
     coefs = lax.all_to_all(wanted, "row", 0, 0)
 
@@ -236,15 +254,17 @@
 
     ham = run(gather_kernel, ((16, 128, 256), BF), ["near"] * 8, hams, limit=LIMIT)
     across = lax.ppermute(ham, "col", cores)
+    across = run(hold_kernel, ((16, 128, 256), BF), ["near"], [across], limit=LIMIT)
+    slab = run(slab_kernel, ((8, 128, 256), BF), ["near", "near"], slabs, limit=LIMIT)
     return pl.pallas_call(
         product_kernel,
         out_shape=jax.ShapeDtypeStruct((1, 2, 128, 128), BF),
-        in_specs=[SMEM] + [VMEM] * 5,
+        in_specs=[SMEM] + [VMEM] * 4,
         out_specs=VMEM,
         scratch_shapes=[pltpu.VMEM((8, 256, 256), BF), pltpu.VMEM((2, 2, 256, 256), BF)],
         compiler_params=pltpu.CompilerParams(vmem_limit_bytes=LIMIT),
         name="product",
-    )(match, near(coefs), near(ham), near(across), near(slabs[0]), near(slabs[1]))
+    )(match, near(coefs), near(ham), near(across), near(slab))
 
 
 def solution(mesh):
@@ -257,4 +277,6 @@
         P("row", "col"),
         P("row", "col"),
     )
-    return jax.shard_map(body, mesh=mesh, in_specs=placed, out_specs=P("row", "col", None, None), check_vma=False)
+    return jax.shard_map(
+        body, mesh=mesh, in_specs=placed, out_specs=P("row", "col", None, None), check_vma=False
+    )

time: 93.7 us -> 95.2 us (1.016)
  the two profiles are of different devices: /device:TPU:1 before, /device:TPU:38 now
where the time goes in v3:
time: 95.2 us; the launch traced here: 94.7 us
  waiting for transfers between devices  33.7 us (35%)
  starting transfers between devices  29.4 us (31%)
  blocking collectives  16.4 us (17%)
  Pallas kernels  12.5 us (13%)
  local copies, waits for them, and re-layouts  1.83 us (2%)
    ppermute x11, waiting for transfers between devices, shift(): return lax.ppermute(value, 'col', pairs)  23.4 us
    all_to_all x1, blocking collectives, body(): got = lax.all_to_all(stamped, 'row', 0, 0)  16.4 us
    ppermute x11, starting transfers between devices, shift(): return lax.ppermute(value, 'col', pairs)  11.7 us
    pallas_call x9, Pallas kernels, run(): pl.pallas_call(kernel, out_shape=[pltpu.VMEM(shape, kind) for shape, kind...  7.71 us
    all_to_all x1, starting transfers between devices, body(): named = lax.all_to_all(names, 'col', 0, 0)  7.45 us
    all_to_all x1, waiting for transfers between devices, body(): picks = lax.all_to_all(picked, 'row', 0, 0)  5.62 us
    all_to_all x1, starting transfers between devices, body(): picks = lax.all_to_all(picked, 'row', 0, 0)  4.86 us
    all_to_all x1, starting transfers between devices, body(): coefs = lax.all_to_all(wanted, 'row', 0, 0)  4.81 us
  transfers between devices with their start and end apart: 16, of which 11 were waited for; matrix products, arithmetic and copies ran while one was open for 0% of the time, Pallas kernels for 7%

profile of v3, /device:TPU:38, one launch (start us, length us, event | category | flops | bytes accessed | tf_op | source)
XLA Modules:
  0.0 94.7 jit_solution(12682799549004940609)
XLA Ops:
  0.7 1.3 %shard_map.73 = bf16[16,8,128]{2,1,0:T(8,128)(2,1)} custom-call(s32[1]{0:T(128)} %bitcast.17.slab_idx, s32[1,2]{1,0:T(1,128)} %pattern.1), custom_call_target="tpu_custom_call" | custom-call | tf_op jit(solution)/shard_map/pallas_call | solution.py:188
  1.9 7.5 %all-to-all-start = ((bf16[16,8,128]{2,1,0:T(8,128)(2,1)}), bf16[16,8,128]{2,1,0:T(8,128)(2,1)S(1)}, u32[]{:S(2)}, u32[]{:S(2)}) async-start(bf16[16,8,128]{2,1,0:T(8,128)(2,1)} %shard_map.73), calls=%async_computation | async-start | bytes 65536 | tf_op jit(solution)/shard_map/all_to_all | solution.py:203
  9.4 2.3 %shard_map.74 = (bf16[16,8,256]{2,1,0:T(8,128)(2,1)S(1)}, bf16[4,128,128]{2,1,0:T(8,128)(2,1)S(1)}) custom-call(bf16[8,4,128,128]{3,2,1,0:T(8,128)(2,1)} %ham.1, bf16[4,1,128,128]{3,2,1,0:T(8,128)(2,1)} %coef.1), custom_call_target="tpu_custom_call" | custom-call | tf_op jit(solution)/shard_map/pallas_call | solution.py:188
  11.7 2.4 %all-to-all-done.named = bf16[16,8,128]{2,1,0:T(8,128)(2,1)S(1)} async-done(((bf16[16,8,128]{2,1,0:T(8,128)(2,1)}), bf16[16,8,128]{2,1,0:T(8,128)(2,1)S(1)}, u32[]{:S(2)}, u32[]{:S(2)}) %all-to-all-start) | async-done | bytes 32800 | tf_op jit(solution)/shard_map/all_to_all | solution.py:203
  14.1 0.8 shard_map.75
  15.0 16.4 %all_to_all.20.got = bf16[16,8,384]{2,1,0:T(8,128)(2,1)S(1)} all-to-all(bf16[16,8,384]{2,1,0:T(8,128)(2,1)S(1)} %shard_map.75), channel_id=1, replica_groups=mesh['row'=16,'col'=16] {'row'}, dimensions={0} | all-to-all | bytes 196608 | tf_op jit(solution)/shard_map/all_to_all | solution.py:220
  31.4 1.0 %shard_map.77 = bf16[16,16,256]{2,1,0:T(8,128)(2,1)} custom-call(bf16[16,8,384]{2,1,0:T(8,128)(2,1)S(1)} %all_to_all.20.got), custom_call_target="tpu_custom_call" | custom-call | tf_op jit(solution)/shard_map/pallas_call | solution.py:188
  32.4 4.9 %all-to-all-start.2 = ((bf16[16,16,256]{2,1,0:T(8,128)(2,1)}), bf16[16,16,256]{2,1,0:T(8,128)(2,1)S(1)}, u32[]{:S(2)}, u32[]{:S(2)}) async-start(bf16[16,16,256]{2,1,0:T(8,128)(2,1)} %shard_map.77), calls=%async_computation.2 | async-start | bytes 262144 | tf_op jit(solution)/shard_map/all_to_all | solution.py:228
  37.3 1.7 %shard_map.76 = bf16[16,256,128]{2,1,0:T(8,128)(2,1)} custom-call(s32[16,128]{1,0:T(8,128)S(1)} %bitcast.18, bf16[4,128,128]{2,1,0:T(8,128)(2,1)S(1)} %get-tuple-element.10.turned), custom_call_target="tpu_custom_call" | custom-call | tf_op jit(solution)/shard_map/pallas_call | solution.py:188
  39.1 5.6 %all-to-all-done.2.got = bf16[16,16,256]{2,1,0:T(8,128)(2,1)S(1)} async-done(((bf16[16,16,256]{2,1,0:T(8,128)(2,1)}), bf16[16,16,256]{2,1,0:T(8,128)(2,1)S(1)}, u32[]{:S(2)}, u32[]{:S(2)}) %all-to-all-start.2) | async-done | bytes 131104 | tf_op jit(solution)/shard_map/all_to_all | solution.py:228
  44.7 4.8 %all-to-all-start.3 = ((bf16[16,256,128]{2,1,0:T(8,128)(2,1)}), bf16[16,256,128]{2,1,0:T(8,128)(2,1)S(1)}, u32[]{:S(2)}, u32[]{:S(2)}) async-start(bf16[16,256,128]{2,1,0:T(8,128)(2,1)} %shard_map.76), calls=%async_computation.3 | async-start | bytes 2097152 | tf_op jit(solution)/shard_map/all_to_all | solution.py:236
  49.5 0.2 shard_map.78.refs_0_
  49.7 3.0 %collective-permute-start = (bf16[16,16,256]{2,1,0:T(8,128)(2,1)S(1)}, bf16[16,16,256]{2,1,0:T(8,128)(2,1)S(1)}, u32[]{:S(2)}, u32[]{:S(2)}) collective-permute-start(bf16[16,16,256]{2,1,0:T(8,128)(2,1)S(1)} %shard_map.78.refs_0_), channel_id=1, source_target_pairs={{0,8},{1,9},{2,10},{3,11},{4,12},{5,13},{6,14},{7,15},{8,0},{9,1},... | collective-permute-start | bytes 393224 | tf_op jit(solution)/shard_map/ppermute | solution.py:176
  52.7 0.6 collective-permute-start.1
  53.3 2.7 %collective-permute-start.3 = (bf16[16,16,256]{2,1,0:T(8,128)(2,1)S(1)}, bf16[16,16,256]{2,1,0:T(8,128)(2,1)S(1)}, u32[]{:S(2)}, u32[]{:S(2)}) collective-permute-start(bf16[16,16,256]{2,1,0:T(8,128)(2,1)S(1)} %shard_map.78.refs_0_), channel_id=1, source_target_pairs={{0,6},{1,7},{2,0},{3,1},{4,2},{5,3},{6,4},{7,5},{8,14},{9,15},{10,... | collective-permute-start | bytes 393224 | tf_op jit(solution)/shard_map/ppermute | solution.py:176
  56.0 1.0 %collective-permute-done.refs_1_ = bf16[16,16,256]{2,1,0:T(8,128)(2,1)S(1)} collective-permute-done((bf16[16,16,256]{2,1,0:T(8,128)(2,1)S(1)}, bf16[16,16,256]{2,1,0:T(8,128)(2,1)S(1)}, u32[]{:S(2)}, u32[]{:S(2)}) %collective-permute-start) | collective-permute-done | bytes 131104 | tf_op jit(solution)/shard_map/ppermute | solution.py:176
  57.0 0.6 collective-permute-start.2
  57.6 2.7 %collective-permute-start.4 = (bf16[16,16,256]{2,1,0:T(8,128)(2,1)S(1)}, bf16[16,16,256]{2,1,0:T(8,128)(2,1)S(1)}, u32[]{:S(2)}, u32[]{:S(2)}) collective-permute-start(bf16[16,16,256]{2,1,0:T(8,128)(2,1)S(1)} %collective-permute-done.refs_1_), channel_id=1, source_target_pairs={{0,6},{1,7},{2,0},{3,1},{4,2},{5,3},{6,4},{7,5},{8,14},{9,15},{10,... | collective-permute-start | bytes 393224 | tf_op jit(solution)/shard_map/ppermute | solution.py:176
  60.3 3.6 %collective-permute-done.1.refs_2_ = bf16[16,16,256]{2,1,0:T(8,128)(2,1)S(1)} collective-permute-done((bf16[16,16,256]{2,1,0:T(8,128)(2,1)S(1)}, bf16[16,16,256]{2,1,0:T(8,128)(2,1)S(1)}, u32[]{:S(2)}, u32[]{:S(2)}) %collective-permute-start.1) | collective-permute-done | bytes 131104 | tf_op jit(solution)/shard_map/ppermute | solution.py:176
  63.9 1.4 %collective-permute-done.2.refs_3_ = bf16[16,16,256]{2,1,0:T(8,128)(2,1)S(1)} collective-permute-done((bf16[16,16,256]{2,1,0:T(8,128)(2,1)S(1)}, bf16[16,16,256]{2,1,0:T(8,128)(2,1)S(1)}, u32[]{:S(2)}, u32[]{:S(2)}) %collective-permute-start.2) | collective-permute-done | bytes 131104 | tf_op jit(solution)/shard_map/ppermute | solution.py:176
  65.3 5.0 %collective-permute-done.6.refs_7_ = bf16[16,16,256]{2,1,0:T(8,128)(2,1)S(1)} collective-permute-done((bf16[16,16,256]{2,1,0:T(8,128)(2,1)S(1)}, bf16[16,16,256]{2,1,0:T(8,128)(2,1)S(1)}, u32[]{:S(2)}, u32[]{:S(2)}) %collective-permute-start.6) | collective-permute-done | bytes 131104 | tf_op jit(solution)/shard_map/ppermute | solution.py:176
  70.6 0.5 collective-permute-start.8
  71.0 2.2 %collective-permute-done.8 = bf16[128,128]{1,0:T(8,128)(2,1)S(1)} collective-permute-done((bf16[128,128]{1,0:T(8,128)(2,1)S(1)}, bf16[128,128]{1,0:T(8,128)(2,1)S(1)}, u32[]{:S(2)}, u32[]{:S(2)}) %collective-permute-start.8) | collective-permute-done | bytes 32800 | tf_op jit(solution)/shard_map/ppermute | solution.py:212
  73.4 1.9 %collective-permute-start.9 = (bf16[2,128,128]{2,1,0:T(8,128)(2,1)S(1)}, bf16[2,128,128]{2,1,0:T(8,128)(2,1)S(1)}, u32[]{:S(2)}, u32[]{:S(2)}) collective-permute-start(bf16[2,128,128]{2,1,0:T(8,128)(2,1)S(1)} %get-tuple-element.14), channel_id=1, source_target_pairs={{0,2},{1,3},{2,4},{3,5},{4,6},{5,7},{6,0},{7,1},{8,10},{9,11},{10,... | collective-permute-start | bytes 196616 | tf_op jit(solution)/shard_map/ppermute | solution.py:176
  75.4 2.8 %collective-permute-done.11 = bf16[2,128,128]{2,1,0:T(8,128)(2,1)S(1)} collective-permute-done((bf16[2,128,128]{2,1,0:T(8,128)(2,1)S(1)}, bf16[2,128,128]{2,1,0:T(8,128)(2,1)S(1)}, u32[]{:S(2)}, u32[]{:S(2)}) %collective-permute-start.11) | collective-permute-done | bytes 65568 | tf_op jit(solution)/shard_map/ppermute | solution.py:176
  78.2 1.1 %collective-permute-done.10 = bf16[2,128,128]{2,1,0:T(8,128)(2,1)S(1)} collective-permute-done((bf16[2,128,128]{2,1,0:T(8,128)(2,1)S(1)}, bf16[2,128,128]{2,1,0:T(8,128)(2,1)S(1)}, u32[]{:S(2)}, u32[]{:S(2)}) %collective-permute-start.10) | collective-permute-done | bytes 65568 | tf_op jit(solution)/shard_map/ppermute | solution.py:176
  79.3 1.3 %collective-permute-done.9 = bf16[2,128,128]{2,1,0:T(8,128)(2,1)S(1)} collective-permute-done((bf16[2,128,128]{2,1,0:T(8,128)(2,1)S(1)}, bf16[2,128,128]{2,1,0:T(8,128)(2,1)S(1)}, u32[]{:S(2)}, u32[]{:S(2)}) %collective-permute-start.9) | collective-permute-done | bytes 65568 | tf_op jit(solution)/shard_map/ppermute | solution.py:176
  80.7 2.3 %match.1 = s32[128]{0:T(128)S(4)} custom-call(s32[128,4]{1,0:T(8,128)S(1)} %fusion.ham_names, s32[16,128]{1,0:T(8,128)S(1)} %bitcast.19), custom_call_target="tpu_custom_call" | custom-call | tf_op jit(solution)/shard_map/match/pallas_call | solution.py:244
  83.0 7.1 %collective-permute-done.12.far_slabs = bf16[4,2,128,128]{3,2,1,0:T(8,128)(2,1)S(1)} collective-permute-done((bf16[4,2,128,128]{3,2,1,0:T(8,128)(2,1)S(1)}, bf16[4,2,128,128]{3,2,1,0:T(8,128)(2,1)S(1)}, u32[]{:S(2)}, u32[]{:S(2)}) %collective-permute-start.12) | collective-permute-done | bytes 262176 | tf_op jit(solution)/shard_map/ppermute | solution.py:176
  90.3 0.8 copy-done
  91.1 1.0 %copy-done.1 = bf16[8,128,256]{2,1,0:T(8,128)(2,1)S(1)} copy-done((bf16[8,128,256]{2,1,0:T(8,128)(2,1)S(1)}, bf16[8,128,256]{2,1,0:T(8,128)(2,1)}, u32[]{:S(2)}) %copy-start.1) | copy-done | bytes 524312
  92.2 2.5 %product.1 = bf16[1,2,128,128]{3,2,1,0:T(8,128)(2,1)} custom-call(s32[128]{0:T(128)S(4)} %match.1, bf16[16,256,128]{2,1,0:T(8,128)(2,1)S(1)} %all-to-all-done.3.coefs, bf16[16,128,256]{2,1,0:T(8,128)(2,1)S(1)} %shard_map.79.ham, bf16[16,128,256]{2,1,0:T(8,128)(2,1)S(1)} %shard_map.80.across, bf16[8,128,256]{2,1,0:T(8,128)(2,1)S(1)} %copy-done.1), custom_call_target="tpu_custom_call" | custom-call | tf_op jit(solution)/shard_map/product/pallas_call | solution.py:259
  (22 shorter events, 0.8 us)
Async XLA Ops:
  1.9 12.2 %all-to-all-start = ((bf16[16,8,128]{2,1,0:T(8,128)(2,1)}), bf16[16,8,128]{2,1,0:T(8,128)(2,1)S(1)}, u32[]{:S(2)}, u32[]{:S(2)}) async-start(bf16[16,8,128]{2,1,0:T(8,128)(2,1)} %shard_map.73), calls=%async_computation | async-start | bytes 65536 | tf_op jit(solution)/shard_map/all_to_all | solution.py:203
  32.4 12.2 %all-to-all-start.2 = ((bf16[16,16,256]{2,1,0:T(8,128)(2,1)}), bf16[16,16,256]{2,1,0:T(8,128)(2,1)S(1)}, u32[]{:S(2)}, u32[]{:S(2)}) async-start(bf16[16,16,256]{2,1,0:T(8,128)(2,1)} %shard_map.77), calls=%async_computation.2 | async-start | bytes 262144 | tf_op jit(solution)/shard_map/all_to_all | solution.py:228
  44.7 46.4 %all-to-all-start.3 = ((bf16[16,256,128]{2,1,0:T(8,128)(2,1)}), bf16[16,256,128]{2,1,0:T(8,128)(2,1)S(1)}, u32[]{:S(2)}, u32[]{:S(2)}) async-start(bf16[16,256,128]{2,1,0:T(8,128)(2,1)} %shard_map.76), calls=%async_computation.3 | async-start | bytes 2097152 | tf_op jit(solution)/shard_map/all_to_all | solution.py:236
  49.7 20.9 %copy-start.2 = (bf16[1,1,128,128]{3,2,1,0:T(8,128)(2,1)S(1)}, bf16[1,1,128,128]{3,2,1,0:T(8,128)(2,1)}, u32[]{:S(2)}) copy-start(bf16[1,1,128,128]{3,2,1,0:T(8,128)(2,1)} %param.11) | copy-start | bytes 98308
  49.7 7.3 %collective-permute-start = (bf16[16,16,256]{2,1,0:T(8,128)(2,1)S(1)}, bf16[16,16,256]{2,1,0:T(8,128)(2,1)S(1)}, u32[]{:S(2)}, u32[]{:S(2)}) collective-permute-start(bf16[16,16,256]{2,1,0:T(8,128)(2,1)S(1)} %shard_map.78.refs_0_), channel_id=1, source_target_pairs={{0,8},{1,9},{2,10},{3,11},{4,12},{5,13},{6,14},{7,15},{8,0},{9,1},... | collective-permute-start | bytes 393224 | tf_op jit(solution)/shard_map/ppermute | solution.py:176
  52.7 11.1 %collective-permute-start.1 = (bf16[16,16,256]{2,1,0:T(8,128)(2,1)S(1)}, bf16[16,16,256]{2,1,0:T(8,128)(2,1)S(1)}, u32[]{:S(2)}, u32[]{:S(2)}) collective-permute-start(bf16[16,16,256]{2,1,0:T(8,128)(2,1)S(1)} %shard_map.78.refs_0_), channel_id=1, source_target_pairs={{0,2},{1,3},{2,4},{3,5},{4,6},{5,7},{6,0},{7,1},{8,10},{9,11},{10,... | collective-permute-start | bytes 393224 | tf_op jit(solution)/shard_map/ppermute | solution.py:176
  53.3 10.6 %collective-permute-start.3 = (bf16[16,16,256]{2,1,0:T(8,128)(2,1)S(1)}, bf16[16,16,256]{2,1,0:T(8,128)(2,1)S(1)}, u32[]{:S(2)}, u32[]{:S(2)}) collective-permute-start(bf16[16,16,256]{2,1,0:T(8,128)(2,1)S(1)} %shard_map.78.refs_0_), channel_id=1, source_target_pairs={{0,6},{1,7},{2,0},{3,1},{4,2},{5,3},{6,4},{7,5},{8,14},{9,15},{10,... | collective-permute-start | bytes 393224 | tf_op jit(solution)/shard_map/ppermute | solution.py:176
  56.0 7.9 %collective-permute-start.5 = (bf16[16,16,256]{2,1,0:T(8,128)(2,1)S(1)}, bf16[16,16,256]{2,1,0:T(8,128)(2,1)S(1)}, u32[]{:S(2)}, u32[]{:S(2)}) collective-permute-start(bf16[16,16,256]{2,1,0:T(8,128)(2,1)S(1)} %shard_map.78.refs_0_), channel_id=1, source_target_pairs={{0,4},{1,5},{2,6},{3,7},{4,0},{5,1},{6,2},{7,3},{8,12},{9,13},{10,... | collective-permute-start | bytes 393224 | tf_op jit(solution)/shard_map/ppermute | solution.py:176
  57.0 8.3 %collective-permute-start.2 = (bf16[16,16,256]{2,1,0:T(8,128)(2,1)S(1)}, bf16[16,16,256]{2,1,0:T(8,128)(2,1)S(1)}, u32[]{:S(2)}, u32[]{:S(2)}) collective-permute-start(bf16[16,16,256]{2,1,0:T(8,128)(2,1)S(1)} %collective-permute-done.refs_1_), channel_id=1, source_target_pairs={{0,2},{1,3},{2,4},{3,5},{4,6},{5,7},{6,0},{7,1},{8,10},{9,11},{10,... | collective-permute-start | bytes 393224 | tf_op jit(solution)/shard_map/ppermute | solution.py:176
  57.6 7.7 %collective-permute-start.4 = (bf16[16,16,256]{2,1,0:T(8,128)(2,1)S(1)}, bf16[16,16,256]{2,1,0:T(8,128)(2,1)S(1)}, u32[]{:S(2)}, u32[]{:S(2)}) collective-permute-start(bf16[16,16,256]{2,1,0:T(8,128)(2,1)S(1)} %collective-permute-done.refs_1_), channel_id=1, source_target_pairs={{0,6},{1,7},{2,0},{3,1},{4,2},{5,3},{6,4},{7,5},{8,14},{9,15},{10,... | collective-permute-start | bytes 393224 | tf_op jit(solution)/shard_map/ppermute | solution.py:176
  63.9 6.5 %collective-permute-start.6 = (bf16[16,16,256]{2,1,0:T(8,128)(2,1)S(1)}, bf16[16,16,256]{2,1,0:T(8,128)(2,1)S(1)}, u32[]{:S(2)}, u32[]{:S(2)}) collective-permute-start(bf16[16,16,256]{2,1,0:T(8,128)(2,1)S(1)} %collective-permute-done.refs_1_), channel_id=1, source_target_pairs={{0,4},{1,5},{2,6},{3,7},{4,0},{5,1},{6,2},{7,3},{8,12},{9,13},{10,... | collective-permute-start | bytes 393224 | tf_op jit(solution)/shard_map/ppermute | solution.py:176
  70.4 20.6 %collective-permute-start.7 = (bf16[16,128,256]{2,1,0:T(8,128)(2,1)S(1)}, bf16[16,128,256]{2,1,0:T(8,128)(2,1)S(1)}, u32[]{:S(2)}, u32[]{:S(2)}) collective-permute-start(bf16[16,128,256]{2,1,0:T(8,128)(2,1)S(1)} %shard_map.79.ham), channel_id=1, source_target_pairs={{0,1},{1,0},{2,3},{3,2},{4,5},{5,4},{6,7},{7,6},{8,9},{9,8},{10,11... | collective-permute-start | bytes 3145736 | tf_op jit(solution)/shard_map/ppermute | solution.py:256
  70.6 2.7 %collective-permute-start.8 = (bf16[128,128]{1,0:T(8,128)(2,1)S(1)}, bf16[128,128]{1,0:T(8,128)(2,1)S(1)}, u32[]{:S(2)}, u32[]{:S(2)}) collective-permute-start(bf16[128,128]{1,0:T(8,128)(2,1)S(1)} %bitcast.23), channel_id=1, source_target_pairs={{0,1},{1,0},{2,3},{3,2},{4,5},{5,4},{6,7},{7,6},{8,9},{9,8},{10,11... | collective-permute-start | bytes 98312 | tf_op jit(solution)/shard_map/ppermute | solution.py:212
  73.3 4.9 %collective-permute-start.11 = (bf16[2,128,128]{2,1,0:T(8,128)(2,1)S(1)}, bf16[2,128,128]{2,1,0:T(8,128)(2,1)S(1)}, u32[]{:S(2)}, u32[]{:S(2)}) collective-permute-start(bf16[2,128,128]{2,1,0:T(8,128)(2,1)S(1)} %get-tuple-element.14), channel_id=1, source_target_pairs={{0,6},{1,7},{2,0},{3,1},{4,2},{5,3},{6,4},{7,5},{8,14},{9,15},{10,... | collective-permute-start | bytes 196616 | tf_op jit(solution)/shard_map/ppermute | solution.py:176
  73.3 6.0 %collective-permute-start.10 = (bf16[2,128,128]{2,1,0:T(8,128)(2,1)S(1)}, bf16[2,128,128]{2,1,0:T(8,128)(2,1)S(1)}, u32[]{:S(2)}, u32[]{:S(2)}) collective-permute-start(bf16[2,128,128]{2,1,0:T(8,128)(2,1)S(1)} %get-tuple-element.14), channel_id=1, source_target_pairs={{0,4},{1,5},{2,6},{3,7},{4,0},{5,1},{6,2},{7,3},{8,12},{9,13},{10,... | collective-permute-start | bytes 196616 | tf_op jit(solution)/shard_map/ppermute | solution.py:176
  73.4 7.1 %collective-permute-start.9 = (bf16[2,128,128]{2,1,0:T(8,128)(2,1)S(1)}, bf16[2,128,128]{2,1,0:T(8,128)(2,1)S(1)}, u32[]{:S(2)}, u32[]{:S(2)}) collective-permute-start(bf16[2,128,128]{2,1,0:T(8,128)(2,1)S(1)} %get-tuple-element.14), channel_id=1, source_target_pairs={{0,2},{1,3},{2,4},{3,5},{4,6},{5,7},{6,0},{7,1},{8,10},{9,11},{10,... | collective-permute-start | bytes 196616 | tf_op jit(solution)/shard_map/ppermute | solution.py:176
  80.6 9.5 %collective-permute-start.12 = (bf16[4,2,128,128]{3,2,1,0:T(8,128)(2,1)S(1)}, bf16[4,2,128,128]{3,2,1,0:T(8,128)(2,1)S(1)}, u32[]{:S(2)}, u32[]{:S(2)}) collective-permute-start(bf16[4,2,128,128]{3,2,1,0:T(8,128)(2,1)S(1)} %pad_maximum_fusion.near_slabs), channel_id=1, source_target_pairs={{0,8},{1,9},{2,10},{3,11},{4,12},{5,13},{6,14},{7,15},{8,0},{9,1},... | collective-permute-start | bytes 786440 | tf_op jit(solution)/shard_map/ppermute | solution.py:176
  90.2 0.8 copy-start
  91.1 1.0 %copy-start.1 = (bf16[8,128,256]{2,1,0:T(8,128)(2,1)S(1)}, bf16[8,128,256]{2,1,0:T(8,128)(2,1)}, u32[]{:S(2)}) copy-start(bf16[8,128,256]{2,1,0:T(8,128)(2,1)} %copy-done) | copy-start | bytes 1572868

commit v4 on v3

--- a/solution.py
+++ b/solution.py
@@ -130,7 +130,7 @@
         ham[:, pl.ds(pl.multiple_of(s * 16, 16), 16), :] = hams[t][...]
 
 
-def slab_kernel(near_slabs, far_slabs, slab):
+def slab_kernel(near_slabs, far_slabs, slab, last):
     col = lax.axis_index("col")
     chip, core = col // 2, col % 2
     x, y = chip // 4, chip % 4
@@ -138,14 +138,18 @@
         d = (y - s % 4 + 4) % 4
         for h in range(2):
             at = (h + core) % 2
-            slab[s, :, 128 * h : 128 * h + 128] = jnp.where(x == s // 4, near_slabs[d, at], far_slabs[d, at])
+            block = jnp.where(x == s // 4, near_slabs[d, at], far_slabs[d, at])
+            if s < 6:
+                slab[s, :, 128 * h : 128 * h + 128] = block
+            else:
+                last[s - 6, :, 128 * h : 128 * h + 128] = block
 
 
 def hold_kernel(across, held):
     held[...] = across[...]
 
 
-def product_kernel(match, coefs, ham, across, slab, out, image, chosen):
+def product_kernel(match, coefs, ham, across, slab, last, out, image, chosen):
     core = lax.axis_index("col") % 2
     for m in range(16):
         for k in range(4):
@@ -161,7 +165,7 @@
         image[m // 2, 128 * (m % 2) : 128 * (m % 2) + 128] = (dot(ham[m], chosen[m % 2, 0]) + dot(across[m], chosen[m % 2, 1])).astype(BF)
     total = jnp.zeros((128, 256), F32)
     for s in range(8):
-        total = total + dot(slab[s], image[s])
+        total = total + dot(slab[s] if s < 6 else last[s - 6], image[s])
     for e in range(2):
         out[0, e] = total[:, e * 128 : e * 128 + 128].astype(BF)
 
@@ -255,16 +259,16 @@
     ham = run(gather_kernel, ((16, 128, 256), BF), ["near"] * 8, hams, limit=LIMIT)
     across = lax.ppermute(ham, "col", cores)
     across = run(hold_kernel, ((16, 128, 256), BF), ["near"], [across], limit=LIMIT)
-    slab = run(slab_kernel, ((8, 128, 256), BF), ["near", "near"], slabs, limit=LIMIT)
+    slab, last = run(slab_kernel, [((6, 128, 256), BF), ((2, 128, 256), BF)], ["near", "near"], slabs, limit=LIMIT)
     return pl.pallas_call(
         product_kernel,
         out_shape=jax.ShapeDtypeStruct((1, 2, 128, 128), BF),
-        in_specs=[SMEM] + [VMEM] * 4,
+        in_specs=[SMEM] + [VMEM] * 5,
         out_specs=VMEM,
         scratch_shapes=[pltpu.VMEM((8, 256, 256), BF), pltpu.VMEM((2, 2, 256, 256), BF)],
         compiler_params=pltpu.CompilerParams(vmem_limit_bytes=LIMIT),
         name="product",
-    )(match, near(coefs), near(ham), near(across), near(slab))
+    )(match, near(coefs), near(ham), near(across), near(slab), last)
 
 
 def solution(mesh):

time: 95.2 us -> 94.9 us (level)
  no operation moved by 1% of the time
where the time goes in v4:
time: 94.9 us; the launch traced here: 94.4 us
  waiting for transfers between devices  33.7 us (36%)
  starting transfers between devices  29.4 us (31%)
  blocking collectives  16.4 us (17%)
  Pallas kernels  12.5 us (13%)
  local copies, waits for them, and re-layouts  1.56 us (2%)
    ppermute x11, waiting for transfers between devices, shift(): return lax.ppermute(value, 'col', pairs)  23.4 us
    all_to_all x1, blocking collectives, body(): got = lax.all_to_all(stamped, 'row', 0, 0)  16.4 us
    ppermute x11, starting transfers between devices, shift(): return lax.ppermute(value, 'col', pairs)  11.7 us
    pallas_call x9, Pallas kernels, run(): pl.pallas_call(kernel, out_shape=[pltpu.VMEM(shape, kind) for shape, kind...  7.72 us
    all_to_all x1, starting transfers between devices, body(): named = lax.all_to_all(names, 'col', 0, 0)  7.45 us
    all_to_all x1, waiting for transfers between devices, body(): picks = lax.all_to_all(picked, 'row', 0, 0)  5.62 us
    all_to_all x1, starting transfers between devices, body(): picks = lax.all_to_all(picked, 'row', 0, 0)  4.86 us
    all_to_all x1, starting transfers between devices, body(): coefs = lax.all_to_all(wanted, 'row', 0, 0)  4.81 us
  transfers between devices with their start and end apart: 16, of which 11 were waited for; matrix products, arithmetic and copies ran while one was open for 0% of the time, Pallas kernels for 7%

profile of v4, /device:TPU:38, one launch (start us, length us, event | category | flops | bytes accessed | tf_op | source)
XLA Modules:
  0.0 94.4 jit_solution(9530756065356463833)
XLA Ops:
  0.7 1.3 %shard_map.73 = bf16[16,8,128]{2,1,0:T(8,128)(2,1)} custom-call(s32[1]{0:T(128)} %bitcast.17.slab_idx, s32[1,2]{1,0:T(1,128)} %pattern.1), custom_call_target="tpu_custom_call" | custom-call | tf_op jit(solution)/shard_map/pallas_call | solution.py:192
  1.9 7.5 %all-to-all-start = ((bf16[16,8,128]{2,1,0:T(8,128)(2,1)}), bf16[16,8,128]{2,1,0:T(8,128)(2,1)S(1)}, u32[]{:S(2)}, u32[]{:S(2)}) async-start(bf16[16,8,128]{2,1,0:T(8,128)(2,1)} %shard_map.73), calls=%async_computation | async-start | bytes 65536 | tf_op jit(solution)/shard_map/all_to_all | solution.py:207
  9.4 2.3 %shard_map.74 = (bf16[16,8,256]{2,1,0:T(8,128)(2,1)S(1)}, bf16[4,128,128]{2,1,0:T(8,128)(2,1)S(1)}) custom-call(bf16[8,4,128,128]{3,2,1,0:T(8,128)(2,1)} %ham.1, bf16[4,1,128,128]{3,2,1,0:T(8,128)(2,1)} %coef.1), custom_call_target="tpu_custom_call" | custom-call | tf_op jit(solution)/shard_map/pallas_call | solution.py:192
  11.7 2.4 %all-to-all-done.named = bf16[16,8,128]{2,1,0:T(8,128)(2,1)S(1)} async-done(((bf16[16,8,128]{2,1,0:T(8,128)(2,1)}), bf16[16,8,128]{2,1,0:T(8,128)(2,1)S(1)}, u32[]{:S(2)}, u32[]{:S(2)}) %all-to-all-start) | async-done | bytes 32800 | tf_op jit(solution)/shard_map/all_to_all | solution.py:207
  14.1 0.8 shard_map.75
  15.0 16.4 %all_to_all.20.got = bf16[16,8,384]{2,1,0:T(8,128)(2,1)S(1)} all-to-all(bf16[16,8,384]{2,1,0:T(8,128)(2,1)S(1)} %shard_map.75), channel_id=1, replica_groups=mesh['row'=16,'col'=16] {'row'}, dimensions={0} | all-to-all | bytes 196608 | tf_op jit(solution)/shard_map/all_to_all | solution.py:224
  31.4 1.1 %shard_map.77 = bf16[16,16,256]{2,1,0:T(8,128)(2,1)} custom-call(bf16[16,8,384]{2,1,0:T(8,128)(2,1)S(1)} %all_to_all.20.got), custom_call_target="tpu_custom_call" | custom-call | tf_op jit(solution)/shard_map/pallas_call | solution.py:192
  32.5 4.9 %all-to-all-start.2 = ((bf16[16,16,256]{2,1,0:T(8,128)(2,1)}), bf16[16,16,256]{2,1,0:T(8,128)(2,1)S(1)}, u32[]{:S(2)}, u32[]{:S(2)}) async-start(bf16[16,16,256]{2,1,0:T(8,128)(2,1)} %shard_map.77), calls=%async_computation.2 | async-start | bytes 262144 | tf_op jit(solution)/shard_map/all_to_all | solution.py:232
  37.3 1.7 %shard_map.76 = bf16[16,256,128]{2,1,0:T(8,128)(2,1)} custom-call(s32[16,128]{1,0:T(8,128)S(1)} %bitcast.18, bf16[4,128,128]{2,1,0:T(8,128)(2,1)S(1)} %get-tuple-element.12.turned), custom_call_target="tpu_custom_call" | custom-call | tf_op jit(solution)/shard_map/pallas_call | solution.py:192
  39.1 5.6 %all-to-all-done.2.got = bf16[16,16,256]{2,1,0:T(8,128)(2,1)S(1)} async-done(((bf16[16,16,256]{2,1,0:T(8,128)(2,1)}), bf16[16,16,256]{2,1,0:T(8,128)(2,1)S(1)}, u32[]{:S(2)}, u32[]{:S(2)}) %all-to-all-start.2) | async-done | bytes 131104 | tf_op jit(solution)/shard_map/all_to_all | solution.py:232
  44.7 4.8 %all-to-all-start.3 = ((bf16[16,256,128]{2,1,0:T(8,128)(2,1)}), bf16[16,256,128]{2,1,0:T(8,128)(2,1)S(1)}, u32[]{:S(2)}, u32[]{:S(2)}) async-start(bf16[16,256,128]{2,1,0:T(8,128)(2,1)} %shard_map.76), calls=%async_computation.3 | async-start | bytes 2097152 | tf_op jit(solution)/shard_map/all_to_all | solution.py:240
  49.5 0.2 shard_map.78.refs_0_
  49.7 3.0 %collective-permute-start = (bf16[16,16,256]{2,1,0:T(8,128)(2,1)S(1)}, bf16[16,16,256]{2,1,0:T(8,128)(2,1)S(1)}, u32[]{:S(2)}, u32[]{:S(2)}) collective-permute-start(bf16[16,16,256]{2,1,0:T(8,128)(2,1)S(1)} %shard_map.78.refs_0_), channel_id=1, source_target_pairs={{0,8},{1,9},{2,10},{3,11},{4,12},{5,13},{6,14},{7,15},{8,0},{9,1},... | collective-permute-start | bytes 393224 | tf_op jit(solution)/shard_map/ppermute | solution.py:180
  52.7 0.6 collective-permute-start.1
  53.3 2.7 %collective-permute-start.3 = (bf16[16,16,256]{2,1,0:T(8,128)(2,1)S(1)}, bf16[16,16,256]{2,1,0:T(8,128)(2,1)S(1)}, u32[]{:S(2)}, u32[]{:S(2)}) collective-permute-start(bf16[16,16,256]{2,1,0:T(8,128)(2,1)S(1)} %shard_map.78.refs_0_), channel_id=1, source_target_pairs={{0,6},{1,7},{2,0},{3,1},{4,2},{5,3},{6,4},{7,5},{8,14},{9,15},{10,... | collective-permute-start | bytes 393224 | tf_op jit(solution)/shard_map/ppermute | solution.py:180
  56.0 1.0 %collective-permute-done.refs_1_ = bf16[16,16,256]{2,1,0:T(8,128)(2,1)S(1)} collective-permute-done((bf16[16,16,256]{2,1,0:T(8,128)(2,1)S(1)}, bf16[16,16,256]{2,1,0:T(8,128)(2,1)S(1)}, u32[]{:S(2)}, u32[]{:S(2)}) %collective-permute-start) | collective-permute-done | bytes 131104 | tf_op jit(solution)/shard_map/ppermute | solution.py:180
  57.0 0.6 collective-permute-start.2
  57.6 2.7 %collective-permute-start.4 = (bf16[16,16,256]{2,1,0:T(8,128)(2,1)S(1)}, bf16[16,16,256]{2,1,0:T(8,128)(2,1)S(1)}, u32[]{:S(2)}, u32[]{:S(2)}) collective-permute-start(bf16[16,16,256]{2,1,0:T(8,128)(2,1)S(1)} %collective-permute-done.refs_1_), channel_id=1, source_target_pairs={{0,6},{1,7},{2,0},{3,1},{4,2},{5,3},{6,4},{7,5},{8,14},{9,15},{10,... | collective-permute-start | bytes 393224 | tf_op jit(solution)/shard_map/ppermute | solution.py:180
  60.3 3.6 %collective-permute-done.1.refs_2_ = bf16[16,16,256]{2,1,0:T(8,128)(2,1)S(1)} collective-permute-done((bf16[16,16,256]{2,1,0:T(8,128)(2,1)S(1)}, bf16[16,16,256]{2,1,0:T(8,128)(2,1)S(1)}, u32[]{:S(2)}, u32[]{:S(2)}) %collective-permute-start.1) | collective-permute-done | bytes 131104 | tf_op jit(solution)/shard_map/ppermute | solution.py:180
  63.9 1.4 %collective-permute-done.2.refs_3_ = bf16[16,16,256]{2,1,0:T(8,128)(2,1)S(1)} collective-permute-done((bf16[16,16,256]{2,1,0:T(8,128)(2,1)S(1)}, bf16[16,16,256]{2,1,0:T(8,128)(2,1)S(1)}, u32[]{:S(2)}, u32[]{:S(2)}) %collective-permute-start.2) | collective-permute-done | bytes 131104 | tf_op jit(solution)/shard_map/ppermute | solution.py:180
  65.3 5.0 %collective-permute-done.6.refs_7_ = bf16[16,16,256]{2,1,0:T(8,128)(2,1)S(1)} collective-permute-done((bf16[16,16,256]{2,1,0:T(8,128)(2,1)S(1)}, bf16[16,16,256]{2,1,0:T(8,128)(2,1)S(1)}, u32[]{:S(2)}, u32[]{:S(2)}) %collective-permute-start.6) | collective-permute-done | bytes 131104 | tf_op jit(solution)/shard_map/ppermute | solution.py:180
  70.6 0.5 collective-permute-start.8
  71.1 2.2 %collective-permute-done.8 = bf16[128,128]{1,0:T(8,128)(2,1)S(1)} collective-permute-done((bf16[128,128]{1,0:T(8,128)(2,1)S(1)}, bf16[128,128]{1,0:T(8,128)(2,1)S(1)}, u32[]{:S(2)}, u32[]{:S(2)}) %collective-permute-start.8) | collective-permute-done | bytes 32800 | tf_op jit(solution)/shard_map/ppermute | solution.py:216
  73.5 1.9 %collective-permute-start.9 = (bf16[2,128,128]{2,1,0:T(8,128)(2,1)S(1)}, bf16[2,128,128]{2,1,0:T(8,128)(2,1)S(1)}, u32[]{:S(2)}, u32[]{:S(2)}) collective-permute-start(bf16[2,128,128]{2,1,0:T(8,128)(2,1)S(1)} %get-tuple-element.18), channel_id=1, source_target_pairs={{0,2},{1,3},{2,4},{3,5},{4,6},{5,7},{6,0},{7,1},{8,10},{9,11},{10,... | collective-permute-start | bytes 196616 | tf_op jit(solution)/shard_map/ppermute | solution.py:180
  75.4 2.8 %collective-permute-done.11 = bf16[2,128,128]{2,1,0:T(8,128)(2,1)S(1)} collective-permute-done((bf16[2,128,128]{2,1,0:T(8,128)(2,1)S(1)}, bf16[2,128,128]{2,1,0:T(8,128)(2,1)S(1)}, u32[]{:S(2)}, u32[]{:S(2)}) %collective-permute-start.11) | collective-permute-done | bytes 65568 | tf_op jit(solution)/shard_map/ppermute | solution.py:180
  78.2 1.1 %collective-permute-done.10 = bf16[2,128,128]{2,1,0:T(8,128)(2,1)S(1)} collective-permute-done((bf16[2,128,128]{2,1,0:T(8,128)(2,1)S(1)}, bf16[2,128,128]{2,1,0:T(8,128)(2,1)S(1)}, u32[]{:S(2)}, u32[]{:S(2)}) %collective-permute-start.10) | collective-permute-done | bytes 65568 | tf_op jit(solution)/shard_map/ppermute | solution.py:180
  79.3 1.3 %collective-permute-done.9 = bf16[2,128,128]{2,1,0:T(8,128)(2,1)S(1)} collective-permute-done((bf16[2,128,128]{2,1,0:T(8,128)(2,1)S(1)}, bf16[2,128,128]{2,1,0:T(8,128)(2,1)S(1)}, u32[]{:S(2)}, u32[]{:S(2)}) %collective-permute-start.9) | collective-permute-done | bytes 65568 | tf_op jit(solution)/shard_map/ppermute | solution.py:180
  80.7 2.3 %match.1 = s32[128]{0:T(128)S(4)} custom-call(s32[128,4]{1,0:T(8,128)S(1)} %fusion.ham_names, s32[16,128]{1,0:T(8,128)S(1)} %bitcast.19), custom_call_target="tpu_custom_call" | custom-call | tf_op jit(solution)/shard_map/match/pallas_call | solution.py:248
  83.0 7.1 %collective-permute-done.12.far_slabs = bf16[4,2,128,128]{3,2,1,0:T(8,128)(2,1)S(1)} collective-permute-done((bf16[4,2,128,128]{3,2,1,0:T(8,128)(2,1)S(1)}, bf16[4,2,128,128]{3,2,1,0:T(8,128)(2,1)S(1)}, u32[]{:S(2)}, u32[]{:S(2)}) %collective-permute-start.12) | collective-permute-done | bytes 262176 | tf_op jit(solution)/shard_map/ppermute | solution.py:180
  90.3 0.7 copy-done
  91.0 0.9 copy-done.1
  91.9 2.5 %product.1 = bf16[1,2,128,128]{3,2,1,0:T(8,128)(2,1)} custom-call(s32[128]{0:T(128)S(4)} %match.1, bf16[16,256,128]{2,1,0:T(8,128)(2,1)S(1)} %all-to-all-done.3.coefs, bf16[16,128,256]{2,1,0:T(8,128)(2,1)S(1)} %shard_map.79.ham, bf16[16,128,256]{2,1,0:T(8,128)(2,1)S(1)} %shard_map.80.across, bf16[6,128,256]{2,1,0:T(8,128)(2,1)S(1)} %get-tuple-element.15.slab, ...), custom_call_target="tpu_custom_call" | custom-call | tf_op jit(solution)/shard_map/product/pallas_call | solution.py:263
  (22 shorter events, 0.8 us)
Async XLA Ops:
  1.9 12.2 %all-to-all-start = ((bf16[16,8,128]{2,1,0:T(8,128)(2,1)}), bf16[16,8,128]{2,1,0:T(8,128)(2,1)S(1)}, u32[]{:S(2)}, u32[]{:S(2)}) async-start(bf16[16,8,128]{2,1,0:T(8,128)(2,1)} %shard_map.73), calls=%async_computation | async-start | bytes 65536 | tf_op jit(solution)/shard_map/all_to_all | solution.py:207
  32.5 12.2 %all-to-all-start.2 = ((bf16[16,16,256]{2,1,0:T(8,128)(2,1)}), bf16[16,16,256]{2,1,0:T(8,128)(2,1)S(1)}, u32[]{:S(2)}, u32[]{:S(2)}) async-start(bf16[16,16,256]{2,1,0:T(8,128)(2,1)} %shard_map.77), calls=%async_computation.2 | async-start | bytes 262144 | tf_op jit(solution)/shard_map/all_to_all | solution.py:232
  44.7 46.3 %all-to-all-start.3 = ((bf16[16,256,128]{2,1,0:T(8,128)(2,1)}), bf16[16,256,128]{2,1,0:T(8,128)(2,1)S(1)}, u32[]{:S(2)}, u32[]{:S(2)}) async-start(bf16[16,256,128]{2,1,0:T(8,128)(2,1)} %shard_map.76), calls=%async_computation.3 | async-start | bytes 2097152 | tf_op jit(solution)/shard_map/all_to_all | solution.py:240
  49.7 20.9 %copy-start.2 = (bf16[1,1,128,128]{3,2,1,0:T(8,128)(2,1)S(1)}, bf16[1,1,128,128]{3,2,1,0:T(8,128)(2,1)}, u32[]{:S(2)}) copy-start(bf16[1,1,128,128]{3,2,1,0:T(8,128)(2,1)} %param.11) | copy-start | bytes 98308
  49.7 7.3 %collective-permute-start = (bf16[16,16,256]{2,1,0:T(8,128)(2,1)S(1)}, bf16[16,16,256]{2,1,0:T(8,128)(2,1)S(1)}, u32[]{:S(2)}, u32[]{:S(2)}) collective-permute-start(bf16[16,16,256]{2,1,0:T(8,128)(2,1)S(1)} %shard_map.78.refs_0_), channel_id=1, source_target_pairs={{0,8},{1,9},{2,10},{3,11},{4,12},{5,13},{6,14},{7,15},{8,0},{9,1},... | collective-permute-start | bytes 393224 | tf_op jit(solution)/shard_map/ppermute | solution.py:180
  52.7 11.1 %collective-permute-start.1 = (bf16[16,16,256]{2,1,0:T(8,128)(2,1)S(1)}, bf16[16,16,256]{2,1,0:T(8,128)(2,1)S(1)}, u32[]{:S(2)}, u32[]{:S(2)}) collective-permute-start(bf16[16,16,256]{2,1,0:T(8,128)(2,1)S(1)} %shard_map.78.refs_0_), channel_id=1, source_target_pairs={{0,2},{1,3},{2,4},{3,5},{4,6},{5,7},{6,0},{7,1},{8,10},{9,11},{10,... | collective-permute-start | bytes 393224 | tf_op jit(solution)/shard_map/ppermute | solution.py:180
  53.3 10.6 %collective-permute-start.3 = (bf16[16,16,256]{2,1,0:T(8,128)(2,1)S(1)}, bf16[16,16,256]{2,1,0:T(8,128)(2,1)S(1)}, u32[]{:S(2)}, u32[]{:S(2)}) collective-permute-start(bf16[16,16,256]{2,1,0:T(8,128)(2,1)S(1)} %shard_map.78.refs_0_), channel_id=1, source_target_pairs={{0,6},{1,7},{2,0},{3,1},{4,2},{5,3},{6,4},{7,5},{8,14},{9,15},{10,... | collective-permute-start | bytes 393224 | tf_op jit(solution)/shard_map/ppermute | solution.py:180
  56.0 7.9 %collective-permute-start.5 = (bf16[16,16,256]{2,1,0:T(8,128)(2,1)S(1)}, bf16[16,16,256]{2,1,0:T(8,128)(2,1)S(1)}, u32[]{:S(2)}, u32[]{:S(2)}) collective-permute-start(bf16[16,16,256]{2,1,0:T(8,128)(2,1)S(1)} %shard_map.78.refs_0_), channel_id=1, source_target_pairs={{0,4},{1,5},{2,6},{3,7},{4,0},{5,1},{6,2},{7,3},{8,12},{9,13},{10,... | collective-permute-start | bytes 393224 | tf_op jit(solution)/shard_map/ppermute | solution.py:180
  57.0 8.3 %collective-permute-start.2 = (bf16[16,16,256]{2,1,0:T(8,128)(2,1)S(1)}, bf16[16,16,256]{2,1,0:T(8,128)(2,1)S(1)}, u32[]{:S(2)}, u32[]{:S(2)}) collective-permute-start(bf16[16,16,256]{2,1,0:T(8,128)(2,1)S(1)} %collective-permute-done.refs_1_), channel_id=1, source_target_pairs={{0,2},{1,3},{2,4},{3,5},{4,6},{5,7},{6,0},{7,1},{8,10},{9,11},{10,... | collective-permute-start | bytes 393224 | tf_op jit(solution)/shard_map/ppermute | solution.py:180
  57.6 7.7 %collective-permute-start.4 = (bf16[16,16,256]{2,1,0:T(8,128)(2,1)S(1)}, bf16[16,16,256]{2,1,0:T(8,128)(2,1)S(1)}, u32[]{:S(2)}, u32[]{:S(2)}) collective-permute-start(bf16[16,16,256]{2,1,0:T(8,128)(2,1)S(1)} %collective-permute-done.refs_1_), channel_id=1, source_target_pairs={{0,6},{1,7},{2,0},{3,1},{4,2},{5,3},{6,4},{7,5},{8,14},{9,15},{10,... | collective-permute-start | bytes 393224 | tf_op jit(solution)/shard_map/ppermute | solution.py:180
  63.9 6.5 %collective-permute-start.6 = (bf16[16,16,256]{2,1,0:T(8,128)(2,1)S(1)}, bf16[16,16,256]{2,1,0:T(8,128)(2,1)S(1)}, u32[]{:S(2)}, u32[]{:S(2)}) collective-permute-start(bf16[16,16,256]{2,1,0:T(8,128)(2,1)S(1)} %collective-permute-done.refs_1_), channel_id=1, source_target_pairs={{0,4},{1,5},{2,6},{3,7},{4,0},{5,1},{6,2},{7,3},{8,12},{9,13},{10,... | collective-permute-start | bytes 393224 | tf_op jit(solution)/shard_map/ppermute | solution.py:180
  70.5 20.5 %collective-permute-start.7 = (bf16[16,128,256]{2,1,0:T(8,128)(2,1)S(1)}, bf16[16,128,256]{2,1,0:T(8,128)(2,1)S(1)}, u32[]{:S(2)}, u32[]{:S(2)}) collective-permute-start(bf16[16,128,256]{2,1,0:T(8,128)(2,1)S(1)} %shard_map.79.ham), channel_id=1, source_target_pairs={{0,1},{1,0},{2,3},{3,2},{4,5},{5,4},{6,7},{7,6},{8,9},{9,8},{10,11... | collective-permute-start | bytes 3145736 | tf_op jit(solution)/shard_map/ppermute | solution.py:260
  70.6 2.7 %collective-permute-start.8 = (bf16[128,128]{1,0:T(8,128)(2,1)S(1)}, bf16[128,128]{1,0:T(8,128)(2,1)S(1)}, u32[]{:S(2)}, u32[]{:S(2)}) collective-permute-start(bf16[128,128]{1,0:T(8,128)(2,1)S(1)} %bitcast.23), channel_id=1, source_target_pairs={{0,1},{1,0},{2,3},{3,2},{4,5},{5,4},{6,7},{7,6},{8,9},{9,8},{10,11... | collective-permute-start | bytes 98312 | tf_op jit(solution)/shard_map/ppermute | solution.py:216
  73.3 4.9 %collective-permute-start.11 = (bf16[2,128,128]{2,1,0:T(8,128)(2,1)S(1)}, bf16[2,128,128]{2,1,0:T(8,128)(2,1)S(1)}, u32[]{:S(2)}, u32[]{:S(2)}) collective-permute-start(bf16[2,128,128]{2,1,0:T(8,128)(2,1)S(1)} %get-tuple-element.18), channel_id=1, source_target_pairs={{0,6},{1,7},{2,0},{3,1},{4,2},{5,3},{6,4},{7,5},{8,14},{9,15},{10,... | collective-permute-start | bytes 196616 | tf_op jit(solution)/shard_map/ppermute | solution.py:180
  73.4 6.0 %collective-permute-start.10 = (bf16[2,128,128]{2,1,0:T(8,128)(2,1)S(1)}, bf16[2,128,128]{2,1,0:T(8,128)(2,1)S(1)}, u32[]{:S(2)}, u32[]{:S(2)}) collective-permute-start(bf16[2,128,128]{2,1,0:T(8,128)(2,1)S(1)} %get-tuple-element.18), channel_id=1, source_target_pairs={{0,4},{1,5},{2,6},{3,7},{4,0},{5,1},{6,2},{7,3},{8,12},{9,13},{10,... | collective-permute-start | bytes 196616 | tf_op jit(solution)/shard_map/ppermute | solution.py:180
  73.5 7.1 %collective-permute-start.9 = (bf16[2,128,128]{2,1,0:T(8,128)(2,1)S(1)}, bf16[2,128,128]{2,1,0:T(8,128)(2,1)S(1)}, u32[]{:S(2)}, u32[]{:S(2)}) collective-permute-start(bf16[2,128,128]{2,1,0:T(8,128)(2,1)S(1)} %get-tuple-element.18), channel_id=1, source_target_pairs={{0,2},{1,3},{2,4},{3,5},{4,6},{5,7},{6,0},{7,1},{8,10},{9,11},{10,... | collective-permute-start | bytes 196616 | tf_op jit(solution)/shard_map/ppermute | solution.py:180
  80.6 9.5 %collective-permute-start.12 = (bf16[4,2,128,128]{3,2,1,0:T(8,128)(2,1)S(1)}, bf16[4,2,128,128]{3,2,1,0:T(8,128)(2,1)S(1)}, u32[]{:S(2)}, u32[]{:S(2)}) collective-permute-start(bf16[4,2,128,128]{3,2,1,0:T(8,128)(2,1)S(1)} %pad_maximum_fusion.near_slabs), channel_id=1, source_target_pairs={{0,8},{1,9},{2,10},{3,11},{4,12},{5,13},{6,14},{7,15},{8,0},{9,1},... | collective-permute-start | bytes 786440 | tf_op jit(solution)/shard_map/ppermute | solution.py:180
  90.3 0.7 copy-start
  91.0 0.9 copy-start.1
